TPU v7x, 256 devices: a whole 4x4x8 slice. The times are simulated.
256 devices in a mesh: rows: 32 (over x, z), cols: 4 (over y), space: 2 (over core).
Axes of the slice: x: 4, y: 4, z: 8, core: 2. Of those that a mesh axis runs over, the one named last changes fastest.
Arguments:
- hamiltonian: float32 [16384, 1536], P(('rows', 'cols', 'space')), may hold values from -1 to 1
- correlation_root: float32 [16384, 1536], P('rows'), may hold values from -1 to 2
- pattern: int32 [512, 48], replicated, may hold values from 0 to 1
- sub_blocks: int32 [512, 16], P(('rows', 'cols', 'space')), may hold values from 0 to 47, as said below
- sub_count: int32 [512], P(('rows', 'cols', 'space')), may hold values from 8 to 16, as said below
Outputs:
- density: float32 [16384, 1536], P(('rows', 'cols', 'space'))
- charges: float32 [16384], P(('rows', 'cols', 'space'))
Inputs may be any that keep to these rules, and one draw needn't show every extreme that they name: `sub_blocks`: row g lists distinct positions; its first entry is 16 + g mod 16, the position of block g itself. `sub_count`: some submatrix has exactly 16 live blocks.
All inputs are finite; a program needn't handle non-finite values.
Results may differ from a plain program's by a relative error of at most 0.0003.
Values sent between devices are 32-bit elements; how exact they have to be, the bound alone decides.
No kernel may reach another device: no remote copies, remote signals or barrier semaphores. Data moves between devices by JAX's collectives and lax.ppermute only.
A program may use at most 128 MiB of HBM per device.

v0:
```python
import jax
import jax.numpy as jnp
from jax import lax
from jax.sharding import PartitionSpec as P

BLK = 32
MAXB = 16


highest = lax.Precision.HIGHEST


def passed_along(value, axis, steps):
    count = lax.axis_size(axis)
    pairs = [(source, (source + steps) % count) for source in range(count)]
    return lax.ppermute(value, axis, pairs)


def sent_together(arrays, axis, dim, along):
    both = jnp.concatenate(arrays, axis=along)
    out, at, finished = (lax.all_gather(both, axis, axis=dim, tiled=True), 0, [])
    for a in arrays:
        finished.append(lax.slice_in_dim(out, at, at + a.shape[along], axis=along))
        at += a.shape[along]
    return tuple(finished)


def multiply(leftside, rightside):
    return jnp.dot(leftside, rightside, precision=highest, preferred_element_type=jnp.float32)


def expand_pattern(pattern_rows):
    weights = pattern_rows.astype(jnp.float32)
    return jnp.repeat(jnp.repeat(weights, BLK, axis=0), BLK, axis=1)


def build_window(panels):
    whole, above_used, below_used = panels
    slab_width = whole.shape[0]
    zero_block = jnp.zeros((slab_width, slab_width), jnp.float32)
    top_rows = jnp.concatenate([above_used, zero_block], axis=1)
    bottom = jnp.concatenate([zero_block, below_used], axis=1)
    return jnp.concatenate([top_rows, whole, bottom], axis=0)


def band_product(leftside, panels):
    whole, above_used, below_used = panels
    slab_width = whole.shape[0]
    middle = multiply(leftside[:, slab_width : 2 * slab_width], whole)
    upper = multiply(leftside[:, :slab_width], above_used)
    lower = multiply(leftside[:, 2 * slab_width :], below_used)
    zero_cols = jnp.zeros((leftside.shape[0], slab_width), jnp.float32)
    return (
        middle
        + jnp.concatenate([upper, zero_cols], axis=1)
        + jnp.concatenate([zero_cols, lower], axis=1)
    )


def panels_of_rows(piece):
    slab_width = piece.shape[1] // 3
    above_piece = passed_along(piece[:, slab_width:], "rows", 1)
    below_piece = passed_along(piece[:, : 2 * slab_width], "rows", -1)
    whole, above_used, below_used = sent_together(
        (piece, above_piece, below_piece), ("cols", "space"), 0, 1
    )
    return (whole, above_used, below_used)


def panels_of_slab(whole, own_start, own_count):
    return panels_of_rows(lax.dynamic_slice_in_dim(whole, own_start, own_count, 0))


def density_rows(local_window, positions, live_count):
    offsets = (positions[:, None] * BLK + jnp.arange(BLK, dtype=jnp.int32)[None, :]).reshape(-1)
    live_cols = jnp.repeat(
        (jnp.arange(MAXB, dtype=jnp.int32) < live_count).astype(jnp.float32), BLK
    )
    assembled = jnp.take(jnp.take(local_window, offsets, axis=0), offsets, axis=1)
    assembled = assembled * live_cols[:, None] * live_cols[None, :]
    symmetric = 0.5 * (assembled + assembled.T)
    live_order = (live_count * BLK).astype(jnp.float32)
    normalizer = jnp.sqrt(live_order) / (2.0 * jnp.sqrt(jnp.sum(symmetric * symmetric) + 1e-06))
    iterate = symmetric * normalizer
    square = multiply(iterate, iterate)
    iterate = 1.5 * iterate - 0.5 * multiply(iterate, square)
    square = multiply(iterate, iterate)
    home_rows = iterate[:BLK]
    home_rows = 1.5 * home_rows - 0.5 * multiply(home_rows, square)
    padded_order = MAXB * BLK
    home_eye = (
        jnp.arange(BLK, dtype=jnp.int32)[:, None]
        == jnp.arange(padded_order, dtype=jnp.int32)[None, :]
    ).astype(jnp.float32)
    home_density = 0.5 * (home_eye - home_rows)
    placement = (
        offsets[:, None] == jnp.arange(local_window.shape[1], dtype=jnp.int32)[None, :]
    ).astype(jnp.float32)
    return multiply(home_density, placement)


def shards(hamiltonian, correlation_root, pattern, sub_blocks, sub_count):
    slab_width = correlation_root.shape[0]
    slab_blocks = slab_width // BLK
    own_count = hamiltonian.shape[0]
    slab_index = lax.axis_index("rows")
    home_index = lax.axis_index(("cols", "space"))
    own_start = home_index * own_count
    slab_pattern = lax.dynamic_slice_in_dim(pattern, slab_index * slab_blocks, slab_blocks, 0)
    slab_mask = expand_pattern(slab_pattern)
    own_mask = lax.dynamic_slice_in_dim(slab_mask, own_start, own_count, 0)
    own_root = lax.dynamic_slice_in_dim(correlation_root, own_start, own_count, 0)
    root_panels = panels_of_slab(correlation_root, own_start, own_count)
    half_done = own_mask * band_product(hamiltonian, root_panels)
    done_panels = panels_of_rows(half_done)
    own_ortho = own_mask * band_product(own_root, done_panels)
    ortho_panels = panels_of_rows(own_ortho)
    ortho_window = build_window(ortho_panels)
    home_parts = [
        density_rows(ortho_window, sub_blocks[index], sub_count[index])
        for index in range(sub_blocks.shape[0])
    ]
    home_density = jnp.concatenate(home_parts, axis=0)
    half_back = own_mask * band_product(home_density, root_panels)
    back_panels = panels_of_rows(half_back)
    density = own_mask * band_product(own_root, back_panels)
    charges = jnp.sum(density, axis=1)
    return (density, charges)


def solution(mesh):
    return jax.shard_map(
        shards,
        mesh=mesh,
        in_specs=(
            P(("rows", "cols", "space"), None),
            P("rows", None),
            P(),
            P(("rows", "cols", "space"), None),
            P(("rows", "cols", "space")),
        ),
        out_specs=(P(("rows", "cols", "space"), None), P(("rows", "cols", "space"))),
        check_vma=False,
    )
```

profile of v0, /device:TPU:1, one launch (start us, length us, event | category | flops | bytes accessed | tf_op | source)
XLA Modules:
  0.0 361.7 jit_solution(11951140808949245803)
XLA Ops:
  8.3 2.5 collective-permute-start
  10.8 6.2 %collective-permute-start.1 = (f32[64,1024]{1,0:T(8,128)S(1)}, f32[64,1024]{1,0:T(8,128)S(1)}, u32[]{:S(2)}, u32[]{:S(2)}) collective-permute-start(f32[64,1024]{1,0:T(8,128)S(1)} %get-tuple-element.7), channel_id=1, source_target_pairs={{0,248},{8,0},{16,8},{24,16},{32,24},{40,32},{48,40},{56,48},{64,5... | collective-permute-start | bytes 786440 | tf_op jit(solution)/shard_map/ppermute | solution.py:16
  18.1 4.9 %collective-permute-done = f32[64,1024]{1,0:T(8,128)S(1)} collective-permute-done((f32[64,1024]{1,0:T(8,128)S(1)}, f32[64,1024]{1,0:T(8,128)S(1)}, u32[]{:S(2)}, u32[]{:S(2)}) %collective-permute-start) | collective-permute-done | bytes 262176 | tf_op jit(solution)/shard_map/ppermute | solution.py:16
  26.2 45.4 %all-gather.5.cloned.1.call-done = f32[512,3584]{1,0:T(8,128)} async-done(((f32[64,3584]{1,0:T(8,128)}), f32[512,3584]{1,0:T(8,128)}) %all-gather.5.cloned.1.call-update) | async-done | bytes 7340048 | tf_op jit(solution)/shard_map/all_gather | solution.py:21
  71.5 3.0 fusion.69
  74.6 3.0 fusion.72
  77.6 4.0 %fusion.46 = f32[64,1536]{1,0:T(8,128)S(1)} fusion(f32[64,1536]{1,0:T(8,128)S(1)} %copy.22, f32[512,3584]{1,0:T(8,128)} %all-gather.5.cloned.1.call-done, f32[64,1024]{1,0:T(8,128)S(1)} %fusion.72, f32[64,1024]{1,0:T(8,128)S(1)} %fusion.69, f32[64,1536]{1,0:T(8,128)S(1)} %copy-done.5), kind=kOutput, calls=%fused_computation.32 | convolution fusion | flops 604274688 | bytes 4587520 | tf_op jit(solution)/shard_map/dot_general | solution.py:29
  83.0 4.0 %collective-permute-start.3 = (f32[64,1024]{1,0:T(8,128)S(1)}, f32[64,1024]{1,0:T(8,128)S(1)}, u32[]{:S(2)}, u32[]{:S(2)}) collective-permute-start(f32[64,1024]{1,0:T(8,128)S(1)} %get-tuple-element.13), channel_id=1, source_target_pairs={{0,248},{8,0},{16,8},{24,16},{32,24},{40,32},{48,40},{56,48},{64,5... | collective-permute-start | bytes 786440 | tf_op jit(solution)/shard_map/ppermute | solution.py:16
  87.0 6.4 %collective-permute-done.2 = f32[64,1024]{1,0:T(8,128)S(1)} collective-permute-done((f32[64,1024]{1,0:T(8,128)S(1)}, f32[64,1024]{1,0:T(8,128)S(1)}, u32[]{:S(2)}, u32[]{:S(2)}) %collective-permute-start.2) | collective-permute-done | bytes 262176 | tf_op jit(solution)/shard_map/ppermute | solution.py:16
  94.5 13.8 %all-gather.9.cloned.1.call-start = ((), (), s32[]{:S(2)}) async-start(), calls=%async_computation.2 | async-start | bytes 8257536 | tf_op jit(solution)/shard_map/all_gather | solution.py:21
  108.4 32.6 %all-gather.7.cloned.1.call-done = f32[512,3584]{1,0:T(8,128)} async-done(((f32[64,3584]{1,0:T(8,128)}), f32[512,3584]{1,0:T(8,128)}) %all-gather.7.cloned.1.call-update) | async-done | bytes 7340048 | tf_op jit(solution)/shard_map/all_gather | solution.py:21
  141.0 3.0 fusion.55
  144.0 3.1 fusion.53
  147.1 4.0 %fusion.31 = f32[64,1536]{1,0:T(8,128)S(1)} fusion(f32[64,1536]{1,0:T(8,128)S(1)} %copy.22, f32[512,3584]{1,0:T(8,128)} %all-gather.7.cloned.1.call-done, f32[64,1024]{1,0:T(8,128)S(1)} %fusion.53, f32[64,1024]{1,0:T(8,128)S(1)} %fusion.55, f32[512,1536]{1,0:T(8,128)} %param.10, s32[]{:T(128)S(6)} %select_n.22, s32[]{:T(128)S(6)} %add.156), kind=kOutput, calls=%fused_computation.27 | convolution fusion | flops 604274688 | bytes 4587528 | tf_op jit(solution)/shard_map/dot_general | solution.py:29
  152.5 4.0 %collective-permute-start.5 = (f32[64,1024]{1,0:T(8,128)S(1)}, f32[64,1024]{1,0:T(8,128)S(1)}, u32[]{:S(2)}, u32[]{:S(2)}) collective-permute-start(f32[64,1024]{1,0:T(8,128)S(1)} %get-tuple-element.11), channel_id=1, source_target_pairs={{0,248},{8,0},{16,8},{24,16},{32,24},{40,32},{48,40},{56,48},{64,5... | collective-permute-start | bytes 786440 | tf_op jit(solution)/shard_map/ppermute | solution.py:16
  156.5 6.4 %collective-permute-done.4 = f32[64,1024]{1,0:T(8,128)S(1)} collective-permute-done((f32[64,1024]{1,0:T(8,128)S(1)}, f32[64,1024]{1,0:T(8,128)S(1)}, u32[]{:S(2)}, u32[]{:S(2)}) %collective-permute-start.4) | collective-permute-done | bytes 262176 | tf_op jit(solution)/shard_map/ppermute | solution.py:16
  169.8 40.7 %all-gather.9.cloned.1.call-done = f32[512,3584]{1,0:T(8,128)} async-done(((f32[64,3584]{1,0:T(8,128)}), f32[512,3584]{1,0:T(8,128)}) %all-gather.9.cloned.1.call-update) | async-done | bytes 7340048 | tf_op jit(solution)/shard_map/all_gather | solution.py:21
  210.5 2.8 fusion.114
  213.3 1.9 slice-done.2
  215.2 4.8 %select_maximum_fusion = f32[1536,1536]{1,0:T(8,128)} fusion(f32[512,1024]{1,0:T(8,128)S(1)} %get-tuple-element.5, f32[512,1024]{1,0:T(8,128)S(1)} %get-tuple-element.4, f32[512,1536]{1,0:T(8,128)S(1)} %slice-done.2), kind=kLoop, calls=%fused_computation.4 | loop fusion | flops 14155776 | bytes 16777216 | tf_op jit(solution)/shard_map/concatenate | solution.py:43
  220.0 7.5 %gather_fusion = f32[512,1536]{1,0:T(8,128)S(1)} fusion(f32[1536,1536]{1,0:T(8,128)} %select_maximum_fusion, s32[1024]{0:T(1024)} %pad_clamp_fusion.1), kind=kCustom, calls=%fused_computation.clone | custom fusion | bytes 6293504 | tf_op jit(solution)/shard_map/jit(_take)/gather | solution.py:79
  227.5 2.5 broadcast_select_fusion.1
  230.0 2.4 copy.18
  232.4 2.5 gather_fusion.1
  234.9 1.5 fusion.82
  236.7 1.7 multiply_reduce_fusion.1
  239.1 1.9 fusion.86
  241.1 2.0 fusion.68
  243.1 1.8 fusion.121
  245.7 2.0 fusion.4
  247.6 7.4 %gather_fusion.2 = f32[512,1536]{1,0:T(8,128)S(1)} fusion(f32[1536,1536]{1,0:T(8,128)} %select_maximum_fusion, s32[1024]{0:T(1024)S(1)} %copy-done.6), kind=kCustom, calls=%fused_computation.2.clone | custom fusion | bytes 6293504 | tf_op jit(solution)/shard_map/jit(_take)/gather | solution.py:79
  255.0 1.9 broadcast_select_fusion
  256.9 2.4 copy.20
  259.3 2.3 gather_fusion.3
  261.7 1.4 fusion.81
  265.4 2.7 multiply_reduce_fusion
  268.9 4.3 %fusion.83 = f32[512,512]{1,0:T(8,128)S(1)} fusion(f32[]{:T(128)S(6)} %mul.184, f32[512,512]{1,0:T(8,128)} %copy.21, f32[512,512]{0,1:T(8,128)} %copy-done), kind=kOutput, calls=%fused_computation.75 | convolution fusion | flops 1611137024 | bytes 3145732 | tf_op jit(solution)/shard_map/dot_general | solution.py:29
  273.2 2.0 fusion.67
  275.2 1.8 fusion.122
  280.5 1.4 fusion.57
  281.9 2.0 fusion.34
  284.0 1.6 collective-permute-start.6
  285.5 4.0 %collective-permute-start.7 = (f32[64,1024]{1,0:T(8,128)S(1)}, f32[64,1024]{1,0:T(8,128)S(1)}, u32[]{:S(2)}, u32[]{:S(2)}) collective-permute-start(f32[64,1024]{1,0:T(8,128)S(1)} %get-tuple-element.9), channel_id=1, source_target_pairs={{0,248},{8,0},{16,8},{24,16},{32,24},{40,32},{48,40},{56,48},{64,5... | collective-permute-start | bytes 786440 | tf_op jit(solution)/shard_map/ppermute | solution.py:16
  289.5 6.4 %collective-permute-done.6 = f32[64,1024]{1,0:T(8,128)S(1)} collective-permute-done((f32[64,1024]{1,0:T(8,128)S(1)}, f32[64,1024]{1,0:T(8,128)S(1)}, u32[]{:S(2)}, u32[]{:S(2)}) %collective-permute-start.6) | collective-permute-done | bytes 262176 | tf_op jit(solution)/shard_map/ppermute | solution.py:16
  297.1 46.4 %all-gather.11.cloned.1.call-done = f32[512,3584]{1,0:T(8,128)} async-done(((f32[64,3584]{1,0:T(8,128)}), f32[512,3584]{1,0:T(8,128)}) %all-gather.11.cloned.1.call-update) | async-done | bytes 7340048 | tf_op jit(solution)/shard_map/all_gather | solution.py:21
  343.5 3.0 fusion.51
  346.6 3.1 fusion.49
  349.6 5.4 %fusion.120 = (f32[64]{0:T(128)}, f32[64,1536]{1,0:T(8,128)}) fusion(f32[64,1536]{1,0:T(8,128)S(1)} %copy.22, f32[64,1024]{1,0:T(8,128)S(1)} %fusion.49, f32[64,1024]{1,0:T(8,128)S(1)} %fusion.51, f32[512,3584]{1,0:T(8,128)} %all-gather.11.cloned.1.call-done, f32[512,1536]{1,0:T(8,128)} %param.10, s32[]{:T(128)S(6)} %select_n.22, s32[]{:T(128)S(6)} %add.156), kind=kOutput, calls=%fused_computation.136 | convolution fusion | flops 604372928 | bytes 4587784 | tf_op jit(solution)/shard_map/dot_general | solution.py:29
  (76 shorter events, 22.5 us)
Async XLA Ops:
  7.2 64.4 %all-gather.5.cloned.1.call-start = ((), (), s32[]{:S(2)}) async-start(), calls=%async_computation | async-start | bytes 8257536 | tf_op jit(solution)/shard_map/all_gather | solution.py:21
  8.3 14.7 %collective-permute-start = (f32[64,1024]{1,0:T(8,128)S(1)}, f32[64,1024]{1,0:T(8,128)S(1)}, u32[]{:S(2)}, u32[]{:S(2)}) collective-permute-start(f32[64,1024]{1,0:T(8,128)S(1)} %get-tuple-element.6), channel_id=1, source_target_pairs={{0,8},{8,16},{16,24},{24,32},{32,40},{40,48},{48,56},{56,64},{64,7... | collective-permute-start | bytes 786440 | tf_op jit(solution)/shard_map/ppermute | solution.py:16
  10.8 12.2 %collective-permute-start.1 = (f32[64,1024]{1,0:T(8,128)S(1)}, f32[64,1024]{1,0:T(8,128)S(1)}, u32[]{:S(2)}, u32[]{:S(2)}) collective-permute-start(f32[64,1024]{1,0:T(8,128)S(1)} %get-tuple-element.7), channel_id=1, source_target_pairs={{0,248},{8,0},{16,8},{24,16},{32,24},{40,32},{48,40},{56,48},{64,5... | collective-permute-start | bytes 786440 | tf_op jit(solution)/shard_map/ppermute | solution.py:16
  24.0 117.0 %all-gather.7.cloned.1.call-start = ((), (), s32[]{:S(2)}) async-start(), calls=%async_computation.1 | async-start | bytes 8257536 | tf_op jit(solution)/shard_map/all_gather | solution.py:21
  25.1 46.5 %copy-start.5 = (f32[64,1536]{1,0:T(8,128)S(1)}, f32[64,1536]{1,0:T(8,128)}, u32[]{:S(2)}) copy-start(f32[64,1536]{1,0:T(8,128)} %param.9) | copy-start | bytes 1179652
  81.7 11.8 %collective-permute-start.2 = (f32[64,1024]{1,0:T(8,128)S(1)}, f32[64,1024]{1,0:T(8,128)S(1)}, u32[]{:S(2)}, u32[]{:S(2)}) collective-permute-start(f32[64,1024]{1,0:T(8,128)S(1)} %get-tuple-element.12), channel_id=1, source_target_pairs={{0,8},{8,16},{16,24},{24,32},{32,40},{40,48},{48,56},{56,64},{64,7... | collective-permute-start | bytes 786440 | tf_op jit(solution)/shard_map/ppermute | solution.py:16
  83.0 10.4 %collective-permute-start.3 = (f32[64,1024]{1,0:T(8,128)S(1)}, f32[64,1024]{1,0:T(8,128)S(1)}, u32[]{:S(2)}, u32[]{:S(2)}) collective-permute-start(f32[64,1024]{1,0:T(8,128)S(1)} %get-tuple-element.13), channel_id=1, source_target_pairs={{0,248},{8,0},{16,8},{24,16},{32,24},{40,32},{48,40},{56,48},{64,5... | collective-permute-start | bytes 786440 | tf_op jit(solution)/shard_map/ppermute | solution.py:16
  94.5 116.0 %all-gather.9.cloned.1.call-start = ((), (), s32[]{:S(2)}) async-start(), calls=%async_computation.2 | async-start | bytes 8257536 | tf_op jit(solution)/shard_map/all_gather | solution.py:21
  147.1 17.0 %copy-start.9 = (s32[2,16]{1,0:T(2,128)S(1)}, s32[2,16]{1,0:T(2,128)}, u32[]{:S(2)}) copy-start(s32[2,16]{1,0:T(2,128)} %param.12) | copy-start | bytes 388
  147.1 17.3 %copy-start.8 = (s32[2]{0:T(128)S(1)}, s32[2]{0:T(128)}, u32[]{:S(2)}) copy-start(s32[2]{0:T(128)} %param.13) | copy-start | bytes 28
  151.2 11.8 %collective-permute-start.4 = (f32[64,1024]{1,0:T(8,128)S(1)}, f32[64,1024]{1,0:T(8,128)S(1)}, u32[]{:S(2)}, u32[]{:S(2)}) collective-permute-start(f32[64,1024]{1,0:T(8,128)S(1)} %get-tuple-element.10), channel_id=1, source_target_pairs={{0,8},{8,16},{16,24},{24,32},{32,40},{40,48},{48,56},{56,64},{64,7... | collective-permute-start | bytes 786440 | tf_op jit(solution)/shard_map/ppermute | solution.py:16
  152.5 10.4 %collective-permute-start.5 = (f32[64,1024]{1,0:T(8,128)S(1)}, f32[64,1024]{1,0:T(8,128)S(1)}, u32[]{:S(2)}, u32[]{:S(2)}) collective-permute-start(f32[64,1024]{1,0:T(8,128)S(1)} %get-tuple-element.11), channel_id=1, source_target_pairs={{0,248},{8,0},{16,8},{24,16},{32,24},{40,32},{48,40},{56,48},{64,5... | collective-permute-start | bytes 786440 | tf_op jit(solution)/shard_map/ppermute | solution.py:16
  164.1 179.5 %all-gather.11.cloned.1.call-start = ((), (), s32[]{:S(2)}) async-start(), calls=%async_computation.3 | async-start | bytes 8257536 | tf_op jit(solution)/shard_map/all_gather | solution.py:21
  213.3 1.9 slice-start.2
  234.9 1.9 copy-start.3
  243.1 4.5 %copy-start.6 = (s32[1024]{0:T(1024)S(1)}, s32[1024]{0:T(1024)}, u32[]{:S(2)}) copy-start(s32[1024]{0:T(1024)} %pad_clamp_fusion) | copy-start | bytes 12292
  247.6 7.4 %copy-start.7 = (pred[512]{0:T(512)(128)(4,1)S(1)}, pred[512]{0:T(512)(128)(4,1)}, u32[]{:S(2)}) copy-start(pred[512]{0:T(512)(128)(4,1)} %get-tuple-element.22) | copy-start | bytes 1540
  263.1 1.0 copy-start
  265.4 13.7 %slice-start = ((s8[7340032]{0:T(1024)(128)(4,1)}), s8[3145728]{0:T(1024)(128)(4,1)S(1)}, s32[]{:S(2)}) async-start(s8[7340032]{0:T(1024)(128)(4,1)} %bitcast.69), calls=%async_computation.4 | async-start | bytes 6291456
  268.9 4.3 %copy-start.1 = (f32[512,512]{0,1:T(8,128)S(1)}, f32[512,512]{0,1:T(8,128)}, u32[]{:S(2)}) copy-start(f32[512,512]{0,1:T(8,128)} %copy-done) | copy-start | bytes 3145732
  268.9 4.3 %copy-start.2 = (f32[512,512]{1,0:T(8,128)S(1)}, f32[512,512]{1,0:T(8,128)}, u32[]{:S(2)}) copy-start(f32[512,512]{1,0:T(8,128)} %copy.21) | copy-start | bytes 3145732
  273.2 5.9 %slice-start.1 = ((s8[7340032]{0:T(1024)(128)(4,1)}), s8[4194304]{0:T(1024)(128)(4,1)S(1)}, s32[]{:S(2)}) async-start(s8[7340032]{0:T(1024)(128)(4,1)} %bitcast.69), calls=%async_computation.5 | async-start | bytes 8388608
  275.2 3.9 %copy-start.4 = (f32[32,1536]{1,0:T(8,128)S(1)}, f32[32,1536]{1,0:T(8,128)}, u32[]{:S(2)}) copy-start(f32[32,1536]{1,0:T(8,128)} %fusion.4) | copy-start | bytes 589828
  284.0 12.0 %collective-permute-start.6 = (f32[64,1024]{1,0:T(8,128)S(1)}, f32[64,1024]{1,0:T(8,128)S(1)}, u32[]{:S(2)}, u32[]{:S(2)}) collective-permute-start(f32[64,1024]{1,0:T(8,128)S(1)} %get-tuple-element.8), channel_id=1, source_target_pairs={{0,8},{8,16},{16,24},{24,32},{32,40},{40,48},{48,56},{56,64},{64,7... | collective-permute-start | bytes 786440 | tf_op jit(solution)/shard_map/ppermute | solution.py:16
  285.5 10.4 %collective-permute-start.7 = (f32[64,1024]{1,0:T(8,128)S(1)}, f32[64,1024]{1,0:T(8,128)S(1)}, u32[]{:S(2)}, u32[]{:S(2)}) collective-permute-start(f32[64,1024]{1,0:T(8,128)S(1)} %get-tuple-element.9), channel_id=1, source_target_pairs={{0,248},{8,0},{16,8},{24,16},{32,24},{40,32},{48,40},{56,48},{64,5... | collective-permute-start | bytes 786440 | tf_op jit(solution)/shard_map/ppermute | solution.py:16
Sparse Core Ops, SparseCore 0:
  24.1 47.3 all-gather.4
  94.7 46.2 all-gather.6
  164.2 46.2 all-gather.8
  297.2 46.2 all-gather.10
where the time goes:
time: 369 us; the launch traced here: 362 us
  waiting for transfers between devices  189 us (51%)
  matrix products  54.9 us (15%)
  starting transfers between devices  38.9 us (11%)
  local copies, waits for them, and re-layouts  36.3 us (10%)
  other arithmetic  24.9 us (7%)
  between operations  17.3 us (5%)
    all_gather x4, waiting for transfers between devices, sent_together(): lax.all_gather(both, axis, axis=dim, tiled=True)  165 us
    dot_general x22, matrix products, multiply(): jnp.dot(leftside, rightside, precision=highest, preferred_element_type=jn...  54.9 us
    ppermute x8, starting transfers between devices, passed_along(): return lax.ppermute(value, axis, pairs)  25 us
    ppermute x8, waiting for transfers between devices, passed_along(): return lax.ppermute(value, axis, pairs)  24.2 us
    gather x2, local copies, waits for them, and re-layouts, density_rows(): jnp.take(local_window, offsets, axis=0)  14.9 us
    all_gather x4, starting transfers between devices, sent_together(): lax.all_gather(both, axis, axis=dim, tiled=True)  13.9 us
  transfers between devices with their start and end apart: 12, of which 8 were waited for; matrix products, arithmetic and copies ran while one was open for 2% of the time, Pallas kernels for 0%

commit v1 on v0

v1 whole, which is shorter than its diff:
```python
import functools

import jax
import jax.numpy as jnp
from jax import lax
from jax.experimental import pallas as pl
from jax.experimental.pallas import tpu as pltpu
from jax.sharding import PartitionSpec as P

BLK = 32
MAXB = 16
SLAB = 512
CHUNK = 64
LANES = 256
ORDER = MAXB * BLK
PIECES = 7 * CHUNK
f32 = jnp.float32
bf16 = jnp.bfloat16
ALL = ("cols", "space")
VMEM = pl.BlockSpec(memory_space=pltpu.VMEM)
SMEM = pl.BlockSpec(memory_space=pltpu.SMEM)
PARAMS = pltpu.CompilerParams(vmem_limit_bytes=56 * 1024 * 1024)


def passed_along(value, axis, steps):
    count = lax.axis_size(axis)
    pairs = [(source, (source + steps) % count) for source in range(count)]
    return lax.ppermute(value, axis, pairs)


def kernel_call(body, shapes, operands, in_specs, scratch=(), flops=0, moved=0):
    return pl.pallas_call(
        body,
        out_shape=shapes,
        in_specs=in_specs,
        out_specs=jax.tree.map(lambda _: VMEM, shapes),
        scratch_shapes=list(scratch),
        compiler_params=PARAMS,
        cost_estimate=pl.CostEstimate(flops=flops, bytes_accessed=moved, transcendentals=0),
    )(*operands)


def split(x):
    high = x.astype(bf16)
    return high, (x - high.astype(f32)).astype(bf16)


def dot3(a, b):
    dot = functools.partial(jnp.dot, preferred_element_type=f32)
    return dot(a[0], b[0]) + (dot(a[0], b[1]) + dot(a[1], b[0]))


def send_parts(full, own, up, down):
    own[...] = full
    up[...] = pltpu.roll(full, LANES - CHUNK, 1)[:, : 2 * CHUNK]
    down[...] = full[:, : 2 * CHUNK]


def window_parts(above, own, below):
    blank = jnp.zeros((SLAB, 2 * CHUNK), f32)
    return (
        jnp.concatenate([above, blank], axis=1),
        own,
        pltpu.roll(jnp.concatenate([below, blank], axis=1), CHUNK, 1),
    )


def split_kernel(root, above, own, below, root_hi, root_lo, win_hi, win_lo):
    root_hi[...], root_lo[...] = split(root[...])
    for k, part in enumerate(window_parts(above[...], own[...], below[...])):
        rows = slice(k * SLAB, (k + 1) * SLAB)
        win_hi[rows, :], win_lo[rows, :] = split(part)


def first_kernel(ham, win_hi, win_lo, mask, own, up, down):
    total = jnp.zeros((SLAB, LANES), f32)
    for k in range(3):
        cut = slice(k * SLAB, (k + 1) * SLAB)
        total += dot3(split(ham[:, cut]), (win_hi[cut, :], win_lo[cut, :]))
    send_parts(total * mask[...], own, up, down)


def root_product(root_hi, root_lo, above, own, below, mask):
    total = jnp.zeros((SLAB, LANES), f32)
    for k, part in enumerate(window_parts(above[...], own[...], below[...])):
        cut = slice(k * SLAB, (k + 1) * SLAB)
        total += dot3((root_hi[:, cut], root_lo[:, cut]), split(part))
    return total * mask[...]


def ortho_kernel(root_hi, root_lo, above, own, below, mask, mine, up, down):
    turned = root_product(root_hi, root_lo, above, own, below, mask).T
    mine[...] = turned[: 3 * CHUNK]
    up[...] = turned[CHUNK : 3 * CHUNK]
    down[...] = turned[: 2 * CHUNK]


def density_kernel(root_hi, root_lo, above, own, below, mask, packed):
    full = root_product(root_hi, root_lo, above, own, below, mask)
    half = CHUNK // 2
    for c in range(SLAB // CHUNK):
        rows = full[c * CHUNK : (c + 1) * CHUNK]
        packed[c, :CHUNK, :] = rows[:, : 2 * CHUNK]
        last = rows[:, 2 * CHUNK :]
        lane = lax.broadcasted_iota(jnp.int32, (half, 2 * CHUNK), 1)
        packed[c, CHUNK:, :] = jnp.where(lane < CHUNK, last[:half], pltpu.roll(last[half:], CHUNK, 1))


def solve_kernel(blocks, counts, gathered, out, assembled):
    lane_block = lax.broadcasted_iota(jnp.int32, (BLK, 128), 1) // BLK
    row_id = lax.broadcasted_iota(jnp.int32, (BLK, ORDER), 0)
    col_id = lax.broadcasted_iota(jnp.int32, (BLK, ORDER), 1)
    for g in range(2):
        live = counts[g]
        spots = []
        for i in range(MAXB):
            p = blocks[g, i]
            panel = p // 16
            tile = pl.multiple_of(((p % 16) // 4) * 128, 128)
            shift = lax.rem((i % 4 - p % 4) * BLK + 128, 128)
            spots.append((panel, tile, shift, i < live))

        def gather_row(k, carry):
            q = blocks[g, k]
            j = q // 16
            base = ((q % 16) // 2) * PIECES + (q % 2) * BLK + j * CHUNK
            starts = (base + 3 * CHUNK, base, base + 4 * CHUNK)
            row_live = k < live
            for t in range(4):
                total = jnp.zeros((BLK, 128), f32)
                for ii in range(4):
                    panel, tile, shift, col_live = spots[t * 4 + ii]
                    start = jnp.where(panel == 0, starts[0], jnp.where(panel == 1, starts[1], starts[2]))
                    start = pl.multiple_of(start, BLK)
                    here = row_live & col_live & (jnp.abs(panel - j) <= 1)
                    block = pltpu.roll(gathered[pl.ds(start, BLK), pl.ds(tile, 128)], shift, 1)
                    total = jnp.where(lane_block == jnp.where(here, ii, 9), block, total)
                assembled[pl.ds(pl.multiple_of(k * BLK, BLK), BLK), t * 128 : (t + 1) * 128] = total
            return carry

        lax.fori_loop(0, MAXB, gather_row, 0)
        whole = assembled[...]
        symmetric = 0.5 * (whole + whole.T)
        squares = jnp.sum(symmetric * symmetric, keepdims=True) + 1e-06
        size = jnp.full((1, 1), live * BLK, jnp.int32).astype(f32)
        iterate = symmetric * (jnp.sqrt(size) / (2.0 * jnp.sqrt(squares)))
        parts = split(iterate)
        square = split(dot3(parts, parts))
        iterate = 1.5 * iterate - 0.5 * dot3(parts, square)
        parts = split(iterate)
        home = iterate[:BLK]
        once = dot3((parts[0][:BLK], parts[1][:BLK]), parts)
        home = 1.5 * home - 0.5 * dot3(split(once), parts)
        out[g * BLK : (g + 1) * BLK, :] = 0.5 * (jnp.where(row_id == col_id, 1.0, 0.0) - home)


def back_kernel(blocks, places, rows, win_hi, win_lo, mask, own, up, down, full, part_hi, part_lo):
    def one_block(e, carry):
        g = places[e]
        for i in range(MAXB):
            source = pl.ds(pl.multiple_of(blocks[g, i] * BLK, BLK), BLK)
            target = slice(i * BLK, (i + 1) * BLK)
            part_hi[target, :] = win_hi[source, :]
            part_lo[target, :] = win_lo[source, :]
        home = split(rows[pl.ds(pl.multiple_of(e * BLK, BLK), BLK), :])
        there = pl.ds(pl.multiple_of(g * BLK, BLK), BLK)
        full[there, :] = dot3(home, (part_hi[...], part_lo[...])) * mask[there, :]
        return carry

    lax.fori_loop(0, SLAB // BLK, one_block, 0)
    send_parts(full[...], own, up, down)


def final_kernel(packed, density, charges):
    half = CHUNK // 2
    first = lax.broadcasted_iota(jnp.int32, (CHUNK, 128), 1) < CHUNK
    total = jnp.zeros((CHUNK, 128), f32)
    for m in range(SLAB // (2 * CHUNK)):
        a, b = packed[2 * m], packed[2 * m + 1]
        ab, bb = a[:CHUNK], b[:CHUNK]
        a2, b2 = a[CHUNK:], b[CHUNK:]
        left = jnp.where(first, ab, pltpu.roll(bb, CHUNK, 1))
        middle = jnp.where(first, pltpu.roll(ab, CHUNK, 1), bb)
        right = jnp.concatenate(
            [
                jnp.where(first[:half], a2, pltpu.roll(b2, CHUNK, 1)),
                jnp.where(first[:half], pltpu.roll(a2, CHUNK, 1), b2),
            ],
            axis=0,
        )
        for j, part in enumerate((left, middle, right)):
            density[:, j * SLAB + m * 128 : j * SLAB + (m + 1) * 128] = part
        total += left + middle + right
    charges[...] = jnp.sum(total, axis=1, keepdims=True)


def shards(hamiltonian, root, pattern, sub_blocks, sub_count):
    sds = jax.ShapeDtypeStruct
    slab = lax.axis_index("rows")
    col, core = lax.axis_index("cols"), lax.axis_index("space")
    home = 2 * col + core
    parts = (sds((SLAB, LANES), f32), sds((SLAB, 2 * CHUNK), f32), sds((SLAB, 2 * CHUNK), f32))
    product = dict(flops=6 * SLAB * 3 * SLAB * LANES, moved=6 << 20)

    with jax.named_scope("inputs"):
        ham = lax.all_gather(hamiltonian, ALL, axis=0, tiled=True)
        pieces = [lax.dynamic_slice(root, (0, j * SLAB + home * CHUNK), (SLAB, CHUNK)) for j in range(3)]
        above = passed_along(jnp.concatenate(pieces[1:], axis=1), "rows", 1)
        below = passed_along(jnp.concatenate(pieces[:2], axis=1), "rows", -1)
        own = jnp.concatenate(pieces + [jnp.zeros((SLAB, CHUNK), f32)], axis=1)
        mask = lax.dynamic_slice(pattern, (slab * 16, 0), (16, 48)).astype(f32).reshape(16, 3, 16)
        mask = lax.dynamic_slice(mask, (0, 0, 2 * home), (16, 3, 2)).reshape(16, 6)
        mask = jnp.pad(mask, ((0, 0), (0, 2)))
        mask = jnp.broadcast_to(mask[:, None, :, None], (16, BLK, 8, BLK)).reshape(SLAB, LANES)
        root_hi, root_lo, win_hi, win_lo = kernel_call(
            split_kernel,
            (sds((SLAB, 3 * SLAB), bf16),) * 2 + (sds((3 * SLAB, LANES), bf16),) * 2,
            (root, above, own, below),
            [VMEM] * 4,
            flops=1 << 22,
            moved=8 << 20,
        )
    with jax.named_scope("half_done"):
        own, up, down = kernel_call(
            first_kernel, parts, (ham, win_hi, win_lo, mask), [VMEM] * 4, **product
        )
        above, below = passed_along(up, "rows", 1), passed_along(down, "rows", -1)
    with jax.named_scope("orthogonal"):
        mine, up, down = kernel_call(
            ortho_kernel,
            (sds((3 * CHUNK, SLAB), f32), sds((2 * CHUNK, SLAB), f32), sds((2 * CHUNK, SLAB), f32)),
            (root_hi, root_lo, above, own, below, mask),
            [VMEM] * 6,
            **product,
        )
        above, below = passed_along(up, "rows", 1), passed_along(down, "rows", -1)
        gathered = lax.all_gather(jnp.concatenate([mine, above, below], axis=0), ALL, axis=0, tiled=True)
    with jax.named_scope("lists"):
        lists, _ = lax.optimization_barrier((sub_blocks, ham[:8, :128]))
        lists = lax.all_gather(lists, ALL, axis=0, tiled=True)
    with jax.named_scope("solve"):
        rows = kernel_call(
            solve_kernel,
            sds((2 * BLK, ORDER), f32),
            (sub_blocks, sub_count, gathered),
            [SMEM, SMEM, VMEM],
            scratch=[pltpu.VMEM((ORDER, ORDER), f32)],
            flops=12 * ORDER**3,
            moved=8 << 20,
        )
    with jax.named_scope("share"):
        near = [rows] + [passed_along(rows, "cols", steps) for steps in (1, -1, 2)]
        far = [passed_along(r, "space", 1) for r in near]
        shared = jnp.concatenate(near + far, axis=0)
        chips = jnp.stack([col, (col + 3) % 4, (col + 1) % 4, (col + 2) % 4])
        order = jnp.concatenate([2 * chips + core, 2 * chips + 1 - core])
        places = (2 * order[:, None] + jnp.arange(2)[None, :]).reshape(-1).astype(jnp.int32)
    with jax.named_scope("half_back"):
        own, up, down = kernel_call(
            back_kernel,
            parts,
            (lists, places, shared, win_hi, win_lo, mask),
            [SMEM, SMEM] + [VMEM] * 4,
            scratch=[
                pltpu.VMEM((SLAB, LANES), f32),
                pltpu.VMEM((ORDER, LANES), bf16),
                pltpu.VMEM((ORDER, LANES), bf16),
            ],
            **product,
        )
        above, below = passed_along(up, "rows", 1), passed_along(down, "rows", -1)
    with jax.named_scope("density"):
        packed = kernel_call(
            density_kernel,
            sds((SLAB // CHUNK, 3 * CHUNK // 2, 2 * CHUNK), f32),
            (root_hi, root_lo, above, own, below, mask),
            [VMEM] * 6,
            **product,
        )
        packed = lax.all_to_all(packed, ALL, 0, 0)
        density, charges = kernel_call(
            final_kernel,
            (sds((CHUNK, 3 * SLAB), f32), sds((CHUNK, 1), f32)),
            (packed,),
            [VMEM],
            flops=1 << 20,
            moved=1 << 20,
        )
    return density, charges.reshape(CHUNK)


def solution(mesh):
    return jax.shard_map(
        shards,
        mesh=mesh,
        in_specs=(
            P(("rows", "cols", "space"), None),
            P("rows", None),
            P(),
            P(("rows", "cols", "space"), None),
            P(("rows", "cols", "space")),
        ),
        out_specs=(P(("rows", "cols", "space"), None), P(("rows", "cols", "space"))),
        check_vma=False,
    )
```

time: 369 us -> 212 us (0.57); the launches traced: 362 us -> 212 us
  waiting for transfers between devices: 189 us -> 85.7 us
  matrix products: 54.9 us -> 0 us
  Pallas kernels: 0 us -> 43.5 us
  local copies, waits for them, and re-layouts: 36.3 us -> 8.75 us
  blocking collectives: 0 us -> 24.8 us
  other arithmetic: 24.9 us -> 6.42 us
  starting transfers between devices: 38.9 us -> 28.2 us
    all_gather x4 -> x2, waiting for transfers between devices: 165 us -> 58.7 us  [the longest x1 46.1 us: shards(): lax.all_gather(jnp.concatenate([mine, above, below], axis=0), ALL, axis=0...]
    dot_general x22 -> x0, matrix products: 54.9 us -> none  [multiply(): jnp.dot(leftside, rightside, precision=highest, preferred_element_type=jn...]
    pallas_call x0 -> x7, Pallas kernels: none -> 43.5 us  [kernel_call(): pl.pallas_call(body, out_shape=shapes, in_specs=in_specs, out_specs=jax.t...]
    gather x4 -> x0, local copies, waits for them, and re-layouts: 19.7 us -> none  [the longest x2 14.9 us: density_rows(): jnp.take(local_window, offsets, axis=0)]
    all_gather x4 -> x2, starting transfers between devices: 13.9 us -> 0.08 us  [the longest x1 0.04 us: shards(): lax.all_gather(jnp.concatenate([mine, above, below], axis=0), ALL, axis=0...]
    all_to_all x0 -> x1, blocking collectives: none -> 13.3 us  [shards(): packed = lax.all_to_all(packed, ALL, 0, 0)]
    all_gather x0 -> x1, blocking collectives: none -> 11.5 us  [shards(): lists = lax.all_gather(lists, ALL, axis=0, tiled=True)]
    slice x8 -> x0, local copies, waits for them, and re-layouts: 6.49 us -> none  [the longest x3 4.69 us: sent_together(): finished.append(lax.slice_in_dim(out, at, at + a.shape[along], axis=along))]
  transfers between devices with their start and end apart: 12 -> 17, of which waited for: 8 -> 9; matrix products, arithmetic and copies ran while one was open for 2% -> 4% of each run, Pallas kernels for 0% -> 3%
where the time goes in v1:
time: 212 us
  waiting for transfers between devices  85.7 us (40%)
  Pallas kernels  43.5 us (21%)
  starting transfers between devices  28.2 us (13%)
  blocking collectives  24.8 us (12%)
  between operations  14.2 us (7%)
  local copies, waits for them, and re-layouts  8.75 us (4%)
  other arithmetic  6.42 us (3%)
    all_gather x1, waiting for transfers between devices, shards(): lax.all_gather(jnp.concatenate([mine, above, below], axis=0), ALL, axis=0...  46.1 us
    pallas_call x7, Pallas kernels, kernel_call(): pl.pallas_call(body, out_shape=shapes, in_specs=in_specs, out_specs=jax.t...  43.5 us
    ppermute x15, starting transfers between devices, passed_along(): return lax.ppermute(value, axis, pairs)  28.1 us
    ppermute x15, waiting for transfers between devices, passed_along(): return lax.ppermute(value, axis, pairs)  26.3 us
    all_to_all x1, blocking collectives, shards(): packed = lax.all_to_all(packed, ALL, 0, 0)  13.3 us
    all_gather x1, waiting for transfers between devices, shards(): ham = lax.all_gather(hamiltonian, ALL, axis=0, tiled=True)  12.6 us
    all_gather x1, blocking collectives, shards(): lists = lax.all_gather(lists, ALL, axis=0, tiled=True)  11.5 us
    unnamed x24, local copies, waits for them, and re-layouts  5.07 us
  transfers between devices with their start and end apart: 17, of which 9 were waited for; matrix products, arithmetic and copies ran while one was open for 4% of the time, Pallas kernels for 3%

profile of v1, /device:TPU:1, one launch (start us, length us, event | category | flops | bytes accessed | tf_op | source)
XLA Modules:
  0.0 211.5 jit_solution(13712697091666305645)
XLA Ops:
  7.2 0.7 all-gather.4.cloned.1.call-update
  8.0 1.4 constant_dynamic-slice_fusion.1
  9.3 1.0 pad_maximum_fusion.2
  10.3 2.5 %collective-permute-start = (f32[512,128]{1,0:T(8,128)}, f32[512,128]{1,0:T(8,128)S(1)}, u32[]{:S(2)}, u32[]{:S(2)}) collective-permute-start(f32[512,128]{1,0:T(8,128)} %get-tuple-element.38), channel_id=1, source_target_pairs={{0,8},{8,16},{16,24},{24,32},{32,40},{40,48},{48,56},{56,64},{64,7... | collective-permute-start | bytes 786440 | tf_op jit(solution)/shard_map/inputs/ppermute | solution.py:28
  12.8 6.1 %collective-permute-start.1 = (f32[512,128]{1,0:T(8,128)}, f32[512,128]{1,0:T(8,128)S(1)}, u32[]{:S(2)}, u32[]{:S(2)}) collective-permute-start(f32[512,128]{1,0:T(8,128)} %get-tuple-element.37), channel_id=1, source_target_pairs={{0,248},{8,0},{16,8},{24,16},{32,24},{40,32},{48,40},{56,48},{64,5... | collective-permute-start | bytes 786440 | tf_op jit(solution)/shard_map/inputs/ppermute | solution.py:28
  18.9 0.8 dynamic-slice_convert_fusion
  19.9 0.2 broadcast_in_dim.5
  20.1 1.4 reshape.67.mask
  21.5 1.0 maximum_maximum_fusion.own
  22.5 2.6 %collective-permute-done.above = f32[512,128]{1,0:T(8,128)S(1)} collective-permute-done((f32[512,128]{1,0:T(8,128)}, f32[512,128]{1,0:T(8,128)S(1)}, u32[]{:S(2)}, u32[]{:S(2)}) %collective-permute-start) | collective-permute-done | bytes 262176 | tf_op jit(solution)/shard_map/inputs/ppermute | solution.py:28
  25.2 0.7 copy-done
  25.9 0.7 copy-done.1
  26.6 5.3 %inputs.1 = (bf16[512,1536]{1,0:T(8,128)(2,1)}, bf16[512,1536]{1,0:T(8,128)(2,1)}, bf16[1536,256]{1,0:T(8,128)(2,1)}, bf16[1536,256]{1,0:T(8,128)(2,1)}) custom-call(f32[512,1536]{1,0:T(8,128)} %root.1, f32[512,128]{1,0:T(8,128)} %copy-done, f32[512,256]{1,0:T(8,128)} %maximum_maximum_fusion.own, f32[512,128]{1,0:T(8,128)} %copy-done.1), custom_call_target="tpu_custom_call" | custom-call | flops 4194304 | bytes 8388608 | tf_op jit(solution)/shard_map/inputs/pallas_call | solution.py:32
  31.9 12.6 %all-gather.4.cloned.1.call-done.ham = f32[512,1536]{1,0:T(8,128)} async-done(((f32[64,1536]{1,0:T(8,128)}), f32[512,1536]{1,0:T(8,128)}) %all-gather.4.cloned.1.call-update) | async-done | bytes 3145744 | tf_op jit(solution)/shard_map/inputs/all_gather | solution.py:206
  44.4 4.8 %half_done.1 = (f32[512,256]{1,0:T(8,128)}, f32[512,128]{1,0:T(8,128)}, f32[512,128]{1,0:T(8,128)}) custom-call(f32[512,1536]{1,0:T(8,128)} %all-gather.4.cloned.1.call-done.ham, bf16[1536,256]{1,0:T(8,128)(2,1)} %get-tuple-element.19.win_hi, bf16[1536,256]{1,0:T(8,128)(2,1)} %get-tuple-element.20.win_lo, f32[512,256]{1,0:T(8,128)} %reshape.67.mask), custom_call_target="tpu_custom_call" | custom-call | flops 1207959552 | bytes 6291456 | tf_op jit(solution)/shard_map/half_done/pallas_call | solution.py:32
  49.2 1.3 collective-permute-start.2
  50.5 3.9 %collective-permute-start.3 = (f32[512,128]{1,0:T(8,128)}, f32[512,128]{1,0:T(8,128)S(1)}, u32[]{:S(2)}, u32[]{:S(2)}) collective-permute-start(f32[512,128]{1,0:T(8,128)} %get-tuple-element.23), channel_id=1, source_target_pairs={{0,248},{8,0},{16,8},{24,16},{32,24},{40,32},{48,40},{56,48},{64,5... | collective-permute-start | bytes 786440 | tf_op jit(solution)/shard_map/half_done/ppermute | solution.py:28
  54.4 6.7 %collective-permute-done.2.above = f32[512,128]{1,0:T(8,128)S(1)} collective-permute-done((f32[512,128]{1,0:T(8,128)}, f32[512,128]{1,0:T(8,128)S(1)}, u32[]{:S(2)}, u32[]{:S(2)}) %collective-permute-start.2) | collective-permute-done | bytes 262176 | tf_op jit(solution)/shard_map/half_done/ppermute | solution.py:28
  61.1 0.7 copy-done.2
  61.8 0.1 copy-done.4
  61.9 4.7 %orthogonal.1 = (f32[192,512]{1,0:T(8,128)}, f32[128,512]{1,0:T(8,128)}, f32[128,512]{1,0:T(8,128)}) custom-call(bf16[512,1536]{1,0:T(8,128)(2,1)} %get-tuple-element.17.root_hi, bf16[512,1536]{1,0:T(8,128)(2,1)} %get-tuple-element.18.root_lo, f32[512,128]{1,0:T(8,128)} %copy-done.2, f32[512,256]{1,0:T(8,128)} %get-tuple-element.22.own, ...), custom_call_target="tpu_custom_call" | custom-call | flops 1207959552 | bytes 6291456 | tf_op jit(solution)/shard_map/orthogonal/pallas_call | solution.py:32
  66.6 4.8 %collective-permute-start.5 = (f32[128,512]{1,0:T(8,128)}, f32[128,512]{1,0:T(8,128)S(1)}, u32[]{:S(2)}, u32[]{:S(2)}) collective-permute-start(f32[128,512]{1,0:T(8,128)} %get-tuple-element.26), channel_id=1, source_target_pairs={{0,248},{8,0},{16,8},{24,16},{32,24},{40,32},{48,40},{56,48},{64,5... | collective-permute-start | bytes 786440 | tf_op jit(solution)/shard_map/orthogonal/ppermute | solution.py:28
  71.4 5.8 %collective-permute-done.4 = f32[128,512]{1,0:T(8,128)S(1)} collective-permute-done((f32[128,512]{1,0:T(8,128)}, f32[128,512]{1,0:T(8,128)S(1)}, u32[]{:S(2)}, u32[]{:S(2)}) %collective-permute-start.4) | collective-permute-done | bytes 262176 | tf_op jit(solution)/shard_map/orthogonal/ppermute | solution.py:28
  77.2 2.0 pad_maximum_fusion
  79.4 46.1 %all-gather.6.cloned.1.call-done.gathered = f32[3584,512]{1,0:T(8,128)} async-done(((f32[448,512]{1,0:T(8,128)}), f32[3584,512]{1,0:T(8,128)}) %all-gather.6.cloned.1.call-update) | async-done | bytes 7340048 | tf_op jit(solution)/shard_map/orthogonal/all_gather | solution.py:237
  125.6 15.4 %solve.1 = f32[64,512]{1,0:T(8,128)} custom-call(s32[2,16]{1,0:T(2,128)} %blocks.1, s32[2]{0:T(128)} %counts.1, f32[3584,512]{1,0:T(8,128)} %all-gather.6.cloned.1.call-done.gathered), custom_call_target="tpu_custom_call" | custom-call | flops 1610612736 | bytes 8388608 | tf_op jit(solution)/shard_map/solve/pallas_call | solution.py:32
  140.9 0.3 collective-permute-start.6
  141.3 0.6 add.93.places
  141.9 11.5 %all-gather = s32[8,2,16]{2,1,0:T(2,128)} all-gather(s32[1,2,16]{2,1,0:T(2,128)S(1)} %bitcast.13), channel_id=1, replica_groups=mesh['rows'=32,'cols'=4,'space'=2] {'cols','space'}, dimensions={0}, use_global_device_ids=true | all-gather | bytes 1152 | tf_op jit(solution)/shard_map/lists/all_gather | solution.py:240
  153.5 0.9 constant_dynamic-update-slice_fusion.7
  154.4 0.7 collective-permute-start.8
  155.1 0.8 collective-permute-start.9
  155.9 2.7 %collective-permute-done.7 = f32[64,512]{1,0:T(8,128)S(1)} collective-permute-done((f32[64,512]{1,0:T(8,128)}, f32[64,512]{1,0:T(8,128)S(1)}, u32[]{:S(2)}, u32[]{:S(2)}) %collective-permute-start.7) | collective-permute-done | bytes 131104 | tf_op jit(solution)/shard_map/share/ppermute | solution.py:28
  158.6 1.6 collective-permute-start.11
  160.2 0.9 collective-permute-done.8
  161.1 1.0 collective-permute-start.12
  162.2 0.9 collective-permute-done.12
  163.1 1.0 copy-done.6
  164.1 6.9 %half_back.1 = (f32[512,256]{1,0:T(8,128)}, f32[512,128]{1,0:T(8,128)}, f32[512,128]{1,0:T(8,128)}) custom-call(s32[16,16]{1,0:T(8,128)} %bitcast.12, s32[16]{0:T(128)} %add.93.places, f32[512,512]{1,0:T(8,128)} %copy-done.6, bf16[1536,256]{1,0:T(8,128)(2,1)} %get-tuple-element.19.win_hi, bf16[1536,256]{1,0:T(8,128)(2,1)} %get-tuple-element.20.win_lo, ...), custom_call_target="tpu_custom_call" | custom-call | flops 1207959552 | bytes 6291456 | tf_op jit(solution)/shard_map/half_back/pallas_call | solution.py:32
  171.1 1.3 collective-permute-start.13
  172.3 3.9 %collective-permute-start.14 = (f32[512,128]{1,0:T(8,128)}, f32[512,128]{1,0:T(8,128)S(1)}, u32[]{:S(2)}, u32[]{:S(2)}) collective-permute-start(f32[512,128]{1,0:T(8,128)} %get-tuple-element.29), channel_id=1, source_target_pairs={{0,248},{8,0},{16,8},{24,16},{32,24},{40,32},{48,40},{56,48},{64,5... | collective-permute-start | bytes 786440 | tf_op jit(solution)/shard_map/half_back/ppermute | solution.py:28
  176.2 6.6 %collective-permute-done.13.above = f32[512,128]{1,0:T(8,128)S(1)} collective-permute-done((f32[512,128]{1,0:T(8,128)}, f32[512,128]{1,0:T(8,128)S(1)}, u32[]{:S(2)}, u32[]{:S(2)}) %collective-permute-start.13) | collective-permute-done | bytes 262176 | tf_op jit(solution)/shard_map/half_back/ppermute | solution.py:28
  182.8 0.7 copy-done.3
  183.5 0.1 copy-done.5
  183.6 4.5 %density.2 = f32[8,96,128]{2,1,0:T(8,128)} custom-call(bf16[512,1536]{1,0:T(8,128)(2,1)} %get-tuple-element.17.root_hi, bf16[512,1536]{1,0:T(8,128)(2,1)} %get-tuple-element.18.root_lo, f32[512,128]{1,0:T(8,128)} %copy-done.3, f32[512,256]{1,0:T(8,128)} %get-tuple-element.28.own, f32[512,128]{1,0:T(8,128)} %copy-done.5, f32[512,256]{1,0:T(8,128)} %reshape.67.mask), custom_call_target="tpu_custom_call" | custom-call | flops 1207959552 | bytes 6291456 | tf_op jit(solution)/shard_map/density/pallas_call | solution.py:32
  188.1 13.3 %all_to_all.5.packed = f32[8,96,128]{2,1,0:T(8,128)} all-to-all(f32[8,96,128]{2,1,0:T(8,128)} %density.2), channel_id=1, replica_groups=mesh['rows'=32,'cols'=4,'space'=2] {'cols','space'}, dimensions={0} | all-to-all | bytes 786432 | tf_op jit(solution)/shard_map/density/all_to_all | solution.py:280
  201.4 1.9 density.3
  203.3 1.4 reduce
  (40 shorter events, 0.6 us)
Async XLA Ops:
  7.2 37.3 %all-gather.4.cloned.1.call-start = ((), (), s32[]{:S(2)}) async-start(), calls=%async_computation.1 | async-start | bytes 3538944 | tf_op jit(solution)/shard_map/inputs/all_gather | solution.py:206
  7.9 117.7 %all-gather.6.cloned.1.call-start = ((), (), s32[]{:S(2)}) async-start(), calls=%async_computation.2 | async-start | bytes 8257536 | tf_op jit(solution)/shard_map/orthogonal/all_gather | solution.py:237
  10.3 14.8 %collective-permute-start = (f32[512,128]{1,0:T(8,128)}, f32[512,128]{1,0:T(8,128)S(1)}, u32[]{:S(2)}, u32[]{:S(2)}) collective-permute-start(f32[512,128]{1,0:T(8,128)} %get-tuple-element.38), channel_id=1, source_target_pairs={{0,8},{8,16},{16,24},{24,32},{32,40},{40,48},{48,56},{56,64},{64,7... | collective-permute-start | bytes 786440 | tf_op jit(solution)/shard_map/inputs/ppermute | solution.py:28
  12.8 12.4 %collective-permute-start.1 = (f32[512,128]{1,0:T(8,128)}, f32[512,128]{1,0:T(8,128)S(1)}, u32[]{:S(2)}, u32[]{:S(2)}) collective-permute-start(f32[512,128]{1,0:T(8,128)} %get-tuple-element.37), channel_id=1, source_target_pairs={{0,248},{8,0},{16,8},{24,16},{32,24},{40,32},{48,40},{56,48},{64,5... | collective-permute-start | bytes 786440 | tf_op jit(solution)/shard_map/inputs/ppermute | solution.py:28
  25.2 0.7 copy-start
  25.9 0.7 copy-start.1
  49.2 11.9 %collective-permute-start.2 = (f32[512,128]{1,0:T(8,128)}, f32[512,128]{1,0:T(8,128)S(1)}, u32[]{:S(2)}, u32[]{:S(2)}) collective-permute-start(f32[512,128]{1,0:T(8,128)} %get-tuple-element.21), channel_id=1, source_target_pairs={{0,8},{8,16},{16,24},{24,32},{32,40},{40,48},{48,56},{56,64},{64,7... | collective-permute-start | bytes 786440 | tf_op jit(solution)/shard_map/half_done/ppermute | solution.py:28
  50.5 10.6 %collective-permute-start.3 = (f32[512,128]{1,0:T(8,128)}, f32[512,128]{1,0:T(8,128)S(1)}, u32[]{:S(2)}, u32[]{:S(2)}) collective-permute-start(f32[512,128]{1,0:T(8,128)} %get-tuple-element.23), channel_id=1, source_target_pairs={{0,248},{8,0},{16,8},{24,16},{32,24},{40,32},{48,40},{56,48},{64,5... | collective-permute-start | bytes 786440 | tf_op jit(solution)/shard_map/half_done/ppermute | solution.py:28
  61.1 0.7 copy-start.2
  61.1 0.8 copy-start.4
  66.6 10.6 %collective-permute-start.4 = (f32[128,512]{1,0:T(8,128)}, f32[128,512]{1,0:T(8,128)S(1)}, u32[]{:S(2)}, u32[]{:S(2)}) collective-permute-start(f32[128,512]{1,0:T(8,128)} %get-tuple-element.25), channel_id=1, source_target_pairs={{0,8},{8,16},{16,24},{24,32},{32,40},{40,48},{48,56},{56,64},{64,7... | collective-permute-start | bytes 786440 | tf_op jit(solution)/shard_map/orthogonal/ppermute | solution.py:28
  66.6 10.6 %collective-permute-start.5 = (f32[128,512]{1,0:T(8,128)}, f32[128,512]{1,0:T(8,128)S(1)}, u32[]{:S(2)}, u32[]{:S(2)}) collective-permute-start(f32[128,512]{1,0:T(8,128)} %get-tuple-element.26), channel_id=1, source_target_pairs={{0,248},{8,0},{16,8},{24,16},{32,24},{40,32},{48,40},{56,48},{64,5... | collective-permute-start | bytes 786440 | tf_op jit(solution)/shard_map/orthogonal/ppermute | solution.py:28
  79.4 62.5 %copy-start.7 = (s32[2,16]{1,0:T(2,128)S(1)}, s32[2,16]{1,0:T(2,128)}, u32[]{:S(2)}) copy-start(s32[2,16]{1,0:T(2,128)} %blocks.1) | copy-start | bytes 388
  140.9 14.9 %collective-permute-start.6 = (f32[64,512]{1,0:T(8,128)}, f32[64,512]{1,0:T(8,128)S(1)}, u32[]{:S(2)}, u32[]{:S(2)}) collective-permute-start(f32[64,512]{1,0:T(8,128)} %solve.1), channel_id=1, source_target_pairs={{0,2},{2,4},{4,6},{6,0},{1,3},{3,5},{5,7},{7,1},{8,10},{10,12},{12... | collective-permute-start | bytes 393224 | tf_op jit(solution)/shard_map/share/ppermute | solution.py:28
  153.5 5.1 %collective-permute-start.7 = (f32[64,512]{1,0:T(8,128)}, f32[64,512]{1,0:T(8,128)S(1)}, u32[]{:S(2)}, u32[]{:S(2)}) collective-permute-start(f32[64,512]{1,0:T(8,128)} %solve.1), channel_id=1, source_target_pairs={{0,6},{2,0},{4,2},{6,4},{1,7},{3,1},{5,3},{7,5},{8,14},{10,8},{12,... | collective-permute-start | bytes 393224 | tf_op jit(solution)/shard_map/share/ppermute | solution.py:28
  154.4 6.7 %collective-permute-start.8 = (f32[64,512]{1,0:T(8,128)}, f32[64,512]{1,0:T(8,128)S(1)}, u32[]{:S(2)}, u32[]{:S(2)}) collective-permute-start(f32[64,512]{1,0:T(8,128)} %solve.1), channel_id=1, source_target_pairs={{0,4},{2,6},{4,0},{6,2},{1,5},{3,7},{5,1},{7,3},{8,12},{10,14},{12... | collective-permute-start | bytes 393224 | tf_op jit(solution)/shard_map/share/ppermute | solution.py:28
  155.1 7.1 %collective-permute-start.9 = (f32[64,512]{1,0:T(8,128)}, f32[64,512]{1,0:T(8,128)S(1)}, u32[]{:S(2)}, u32[]{:S(2)}) collective-permute-start(f32[64,512]{1,0:T(8,128)} %solve.1), channel_id=1, source_target_pairs={{0,1},{1,0},{2,3},{3,2},{4,5},{5,4},{6,7},{7,6},{8,9},{9,8},{10,11... | collective-permute-start | bytes 393224 | tf_op jit(solution)/shard_map/share/ppermute | solution.py:28
  155.9 6.3 %collective-permute-start.10 = (f32[64,512]{1,0:T(8,128)S(1)}, f32[64,512]{1,0:T(8,128)S(1)}, u32[]{:S(2)}, u32[]{:S(2)}) collective-permute-start(f32[64,512]{1,0:T(8,128)S(1)} %collective-permute-done.6), channel_id=1, source_target_pairs={{0,1},{1,0},{2,3},{3,2},{4,5},{5,4},{6,7},{7,6},{8,9},{9,8},{10,11... | collective-permute-start | bytes 393224 | tf_op jit(solution)/shard_map/share/ppermute | solution.py:28
  158.6 3.6 %collective-permute-start.11 = (f32[64,512]{1,0:T(8,128)S(1)}, f32[64,512]{1,0:T(8,128)S(1)}, u32[]{:S(2)}, u32[]{:S(2)}) collective-permute-start(f32[64,512]{1,0:T(8,128)S(1)} %collective-permute-done.7), channel_id=1, source_target_pairs={{0,1},{1,0},{2,3},{3,2},{4,5},{5,4},{6,7},{7,6},{8,9},{9,8},{10,11... | collective-permute-start | bytes 393224 | tf_op jit(solution)/shard_map/share/ppermute | solution.py:28
  161.1 2.0 collective-permute-start.12
  163.1 1.0 copy-start.6
  171.1 11.7 %collective-permute-start.13 = (f32[512,128]{1,0:T(8,128)}, f32[512,128]{1,0:T(8,128)S(1)}, u32[]{:S(2)}, u32[]{:S(2)}) collective-permute-start(f32[512,128]{1,0:T(8,128)} %get-tuple-element.27), channel_id=1, source_target_pairs={{0,8},{8,16},{16,24},{24,32},{32,40},{40,48},{48,56},{56,64},{64,7... | collective-permute-start | bytes 786440 | tf_op jit(solution)/shard_map/half_back/ppermute | solution.py:28
  172.3 10.5 %collective-permute-start.14 = (f32[512,128]{1,0:T(8,128)}, f32[512,128]{1,0:T(8,128)S(1)}, u32[]{:S(2)}, u32[]{:S(2)}) collective-permute-start(f32[512,128]{1,0:T(8,128)} %get-tuple-element.29), channel_id=1, source_target_pairs={{0,248},{8,0},{16,8},{24,16},{32,24},{40,32},{48,40},{56,48},{64,5... | collective-permute-start | bytes 786440 | tf_op jit(solution)/shard_map/half_back/ppermute | solution.py:28
  182.8 0.7 copy-start.3
  182.8 0.8 copy-start.5
Sparse Core Ops, SparseCore 0:
  9.8 34.5 all-gather.3
  79.4 46.1 all-gather.5

commit v2 on v1

--- a/solution.py
+++ b/solution.py
@@ -13,7 +13,8 @@
 CHUNK = 64
 LANES = 256
 ORDER = MAXB * BLK
-PIECES = 7 * CHUNK
+OWN_ROWS = 3 * SLAB
+NEAR = 4 * CHUNK
 f32 = jnp.float32
 bf16 = jnp.bfloat16
 ALL = ("cols", "space")
@@ -106,7 +107,18 @@
         packed[c, CHUNK:, :] = jnp.where(lane < CHUNK, last[:half], pltpu.roll(last[half:], CHUNK, 1))
 
 
-def solve_kernel(blocks, counts, gathered, out, assembled):
+def solve_kernel(blocks, counts, slots, own, *rest):
+    near, (out, gathered, assembled, sems) = rest[:-4], rest[-4:]
+    copies = [pltpu.make_async_copy(own, gathered.at[pl.ds(0, OWN_ROWS)], sems.at[0])]
+    at = OWN_ROWS
+    for n, piece in enumerate(near):
+        target = gathered.at[pl.ds(at, piece.shape[0])]
+        copies.append(pltpu.make_async_copy(piece, target, sems.at[n + 1]))
+        at += piece.shape[0]
+    for copy in copies:
+        copy.start()
+    for copy in copies:
+        copy.wait()
     lane_block = lax.broadcasted_iota(jnp.int32, (BLK, 128), 1) // BLK
     row_id = lax.broadcasted_iota(jnp.int32, (BLK, ORDER), 0)
     col_id = lax.broadcasted_iota(jnp.int32, (BLK, ORDER), 1)
@@ -123,8 +135,10 @@
         def gather_row(k, carry):
             q = blocks[g, k]
             j = q // 16
-            base = ((q % 16) // 2) * PIECES + (q % 2) * BLK + j * CHUNK
-            starts = (base + 3 * CHUNK, base, base + 4 * CHUNK)
+            c = (q % 16) // 2
+            base = (q % 2) * BLK + j * CHUNK
+            away = OWN_ROWS + slots[c] * NEAR + base
+            starts = (away, c * 3 * CHUNK + base, away + CHUNK)
             row_live = k < live
             for t in range(4):
                 total = jnp.zeros((BLK, 128), f32)
@@ -191,7 +205,7 @@
         for j, part in enumerate((left, middle, right)):
             density[:, j * SLAB + m * 128 : j * SLAB + (m + 1) * 128] = part
         total += left + middle + right
-    charges[...] = jnp.sum(total, axis=1, keepdims=True)
+    charges[...] = jnp.sum(total.T, axis=0, keepdims=True)
 
 
 def shards(hamiltonian, root, pattern, sub_blocks, sub_count):
@@ -220,6 +234,8 @@
             flops=1 << 22,
             moved=8 << 20,
         )
+        lists = lax.all_gather(sub_blocks, ALL, axis=0, tiled=True)
+        win_hi, lists = lax.optimization_barrier((win_hi, lists))
     with jax.named_scope("half_done"):
         own, up, down = kernel_call(
             first_kernel, parts, (ham, win_hi, win_lo, mask), [VMEM] * 4, **product
@@ -234,17 +250,28 @@
             **product,
         )
         above, below = passed_along(up, "rows", 1), passed_along(down, "rows", -1)
-        gathered = lax.all_gather(jnp.concatenate([mine, above, below], axis=0), ALL, axis=0, tiled=True)
-    with jax.named_scope("lists"):
-        lists, _ = lax.optimization_barrier((sub_blocks, ham[:8, :128]))
-        lists = lax.all_gather(lists, ALL, axis=0, tiled=True)
+        whole = lax.all_gather(mine, ALL, axis=0, tiled=True)
+        near = jnp.concatenate([above, below], axis=0)
+        before, after = passed_along(near, "cols", 1), passed_along(near, "cols", -1)
+        half = NEAR // 2
+        opposite = (passed_along(before[:half], "cols", 1), passed_along(after[half:], "cols", -1))
+        near = (near, before, after) + opposite
+        near = near + tuple(passed_along(piece, "space", 1) for piece in near)
+        steps = jnp.arange(SLAB // CHUNK)
+        turn = lax.rem(steps // 2 - col + 4, 4)
+        slots = jnp.where(turn == 3, 1, jnp.where(turn == 0, 0, turn + 1))
+        slots = (slots + 4 * lax.rem(steps + core, 2)).astype(jnp.int32)
     with jax.named_scope("solve"):
         rows = kernel_call(
             solve_kernel,
             sds((2 * BLK, ORDER), f32),
-            (sub_blocks, sub_count, gathered),
-            [SMEM, SMEM, VMEM],
-            scratch=[pltpu.VMEM((ORDER, ORDER), f32)],
+            (sub_blocks, sub_count, slots, whole) + near,
+            [SMEM] * 3 + [pl.BlockSpec(memory_space=pl.ANY)] * 11,
+            scratch=[
+                pltpu.VMEM((OWN_ROWS + 8 * NEAR, SLAB), f32),
+                pltpu.VMEM((ORDER, ORDER), f32),
+                pltpu.SemaphoreType.DMA((11,)),
+            ],
             flops=12 * ORDER**3,
             moved=8 << 20,
         )
@@ -280,7 +307,7 @@
         packed = lax.all_to_all(packed, ALL, 0, 0)
         density, charges = kernel_call(
             final_kernel,
-            (sds((CHUNK, 3 * SLAB), f32), sds((CHUNK, 1), f32)),
+            (sds((CHUNK, 3 * SLAB), f32), sds((1, CHUNK), f32)),
             (packed,),
             [VMEM],
             flops=1 << 20,

time: 212 us -> 193 us (0.910)
  waiting for transfers between devices: 85.7 us -> 52.4 us
  starting transfers between devices: 28.2 us -> 40 us
  local copies, waits for them, and re-layouts: 8.75 us -> 12.7 us
  other arithmetic: 6.42 us -> 3.63 us
    all_gather x1, waiting for transfers between devices: 46.1 us -> 0.01 us  [shards(): whole = lax.all_gather(mine, ALL, axis=0, tiled=True)]
    ppermute x15 -> x24, waiting for transfers between devices: 26.3 us -> 48.9 us  [passed_along(): return lax.ppermute(value, axis, pairs)]
    ppermute x15 -> x24, starting transfers between devices: 28.1 us -> 40 us  [passed_along(): return lax.ppermute(value, axis, pairs)]
    all_gather x1, waiting for transfers between devices: 12.6 us -> 2.74 us  [shards(): ham = lax.all_gather(hamiltonian, ALL, axis=0, tiled=True)]
    unnamed x24 -> x43, local copies, waits for them, and re-layouts: 5.07 us -> 7.34 us
  transfers between devices with their start and end apart: 17 -> 26, of which waited for: 9 -> 10; matrix products, arithmetic and copies ran while one was open for 4% -> 5% of each run, Pallas kernels for 3% -> 3%
where the time goes in v2:
time: 193 us
  waiting for transfers between devices  52.4 us (27%)
  Pallas kernels  44.1 us (23%)
  starting transfers between devices  40 us (21%)
  blocking collectives  25.5 us (13%)
  between operations  14.3 us (7%)
  local copies, waits for them, and re-layouts  12.7 us (7%)
  other arithmetic  3.63 us (2%)
    ppermute x24, waiting for transfers between devices, passed_along(): return lax.ppermute(value, axis, pairs)  48.9 us
    pallas_call x7, Pallas kernels, kernel_call(): pl.pallas_call(body, out_shape=shapes, in_specs=in_specs, out_specs=jax.t...  44.1 us
    ppermute x24, starting transfers between devices, passed_along(): return lax.ppermute(value, axis, pairs)  40 us
    all_to_all x1, blocking collectives, shards(): packed = lax.all_to_all(packed, ALL, 0, 0)  13.2 us
    all_gather x1, blocking collectives, shards(): lists = lax.all_gather(sub_blocks, ALL, axis=0, tiled=True)  12.3 us
    unnamed x43, local copies, waits for them, and re-layouts  7.34 us
  transfers between devices with their start and end apart: 26, of which 10 were waited for; matrix products, arithmetic and copies ran while one was open for 5% of the time, Pallas kernels for 3%

profile of v2, /device:TPU:1, one launch (start us, length us, event | category | flops | bytes accessed | tf_op | source)
XLA Modules:
  0.0 192.7 jit_solution(8884636589192916180)
XLA Ops:
  7.2 0.7 all-gather.4.cloned.1.call-update
  8.0 1.4 constant_dynamic-slice_fusion.1
  9.4 1.0 pad_maximum_fusion.1
  10.3 8.6 %collective-permute-start.1 = (f32[512,128]{1,0:T(8,128)}, f32[512,128]{1,0:T(8,128)S(1)}, u32[]{:S(2)}, u32[]{:S(2)}) collective-permute-start(f32[512,128]{1,0:T(8,128)} %get-tuple-element.41), channel_id=1, source_target_pairs={{0,248},{8,0},{16,8},{24,16},{32,24},{40,32},{48,40},{56,48},{64,5... | collective-permute-start | bytes 786440 | tf_op jit(solution)/shard_map/inputs/ppermute | solution.py:29
  18.9 0.8 dynamic-slice_convert_fusion
  20.1 1.4 reshape.67.mask
  21.6 12.3 %all-gather = s32[8,2,16]{2,1,0:T(2,128)} all-gather(s32[1,2,16]{2,1,0:T(2,128)S(1)} %bitcast.14), channel_id=1, replica_groups=mesh['rows'=32,'cols'=4,'space'=2] {'cols','space'}, dimensions={0}, use_global_device_ids=true | all-gather | bytes 1152 | tf_op jit(solution)/shard_map/inputs/all_gather | solution.py:237
  33.9 1.0 maximum_maximum_fusion.own
  35.0 0.7 copy-done.7
  35.7 0.7 copy-done.8
  36.4 5.3 %inputs.1 = (bf16[512,1536]{1,0:T(8,128)(2,1)}, bf16[512,1536]{1,0:T(8,128)(2,1)}, bf16[1536,256]{1,0:T(8,128)(2,1)}, bf16[1536,256]{1,0:T(8,128)(2,1)}) custom-call(f32[512,1536]{1,0:T(8,128)} %root.1, f32[512,128]{1,0:T(8,128)} %copy-done.8, f32[512,256]{1,0:T(8,128)} %maximum_maximum_fusion.own, f32[512,128]{1,0:T(8,128)} %copy-done.7), custom_call_target="tpu_custom_call" | custom-call | flops 4194304 | bytes 8388608 | tf_op jit(solution)/shard_map/inputs/pallas_call | solution.py:33
  41.7 2.7 %all-gather.4.cloned.1.call-done.ham = f32[512,1536]{1,0:T(8,128)} async-done(((f32[64,1536]{1,0:T(8,128)}), f32[512,1536]{1,0:T(8,128)}) %all-gather.4.cloned.1.call-update) | async-done | bytes 3145744 | tf_op jit(solution)/shard_map/inputs/all_gather | solution.py:220
  44.4 4.8 %half_done.1 = (f32[512,256]{1,0:T(8,128)}, f32[512,128]{1,0:T(8,128)}, f32[512,128]{1,0:T(8,128)}) custom-call(f32[512,1536]{1,0:T(8,128)} %all-gather.4.cloned.1.call-done.ham, bf16[1536,256]{1,0:T(8,128)(2,1)} %get-tuple-element.23.win_hi, bf16[1536,256]{1,0:T(8,128)(2,1)} %get-tuple-element.24.win_lo, f32[512,256]{1,0:T(8,128)} %reshape.67.mask), custom_call_target="tpu_custom_call" | custom-call | flops 1207959552 | bytes 6291456 | tf_op jit(solution)/shard_map/half_done/pallas_call | solution.py:33
  49.2 1.2 collective-permute-start.2
  50.5 3.9 %collective-permute-start.3 = (f32[512,128]{1,0:T(8,128)}, f32[512,128]{1,0:T(8,128)S(1)}, u32[]{:S(2)}, u32[]{:S(2)}) collective-permute-start(f32[512,128]{1,0:T(8,128)} %get-tuple-element.27), channel_id=1, source_target_pairs={{0,248},{8,0},{16,8},{24,16},{32,24},{40,32},{48,40},{56,48},{64,5... | collective-permute-start | bytes 786440 | tf_op jit(solution)/shard_map/half_done/ppermute | solution.py:29
  54.4 6.7 %collective-permute-done.2.above = f32[512,128]{1,0:T(8,128)S(1)} collective-permute-done((f32[512,128]{1,0:T(8,128)}, f32[512,128]{1,0:T(8,128)S(1)}, u32[]{:S(2)}, u32[]{:S(2)}) %collective-permute-start.2) | collective-permute-done | bytes 262176 | tf_op jit(solution)/shard_map/half_done/ppermute | solution.py:29
  61.1 0.7 copy-done.11
  61.9 4.7 %orthogonal.1 = (f32[192,512]{1,0:T(8,128)}, f32[128,512]{1,0:T(8,128)}, f32[128,512]{1,0:T(8,128)}) custom-call(bf16[512,1536]{1,0:T(8,128)(2,1)} %get-tuple-element.19.root_hi, bf16[512,1536]{1,0:T(8,128)(2,1)} %get-tuple-element.20.root_lo, f32[512,128]{1,0:T(8,128)} %copy-done.11, f32[512,256]{1,0:T(8,128)} %get-tuple-element.26.own, ...), custom_call_target="tpu_custom_call" | custom-call | flops 1207959552 | bytes 6291456 | tf_op jit(solution)/shard_map/orthogonal/pallas_call | solution.py:33
  66.7 4.8 %collective-permute-start.5 = (f32[128,512]{1,0:T(8,128)}, f32[128,512]{1,0:T(8,128)S(1)}, u32[]{:S(2)}, u32[]{:S(2)}) collective-permute-start(f32[128,512]{1,0:T(8,128)} %get-tuple-element.30), channel_id=1, source_target_pairs={{0,248},{8,0},{16,8},{24,16},{32,24},{40,32},{48,40},{56,48},{64,5... | collective-permute-start | bytes 786440 | tf_op jit(solution)/shard_map/orthogonal/ppermute | solution.py:29
  71.5 5.8 %collective-permute-done.4 = f32[128,512]{1,0:T(8,128)S(1)} collective-permute-done((f32[128,512]{1,0:T(8,128)}, f32[128,512]{1,0:T(8,128)S(1)}, u32[]{:S(2)}, u32[]{:S(2)}) %collective-permute-start.4) | collective-permute-done | bytes 262176 | tf_op jit(solution)/shard_map/orthogonal/ppermute | solution.py:29
  77.4 1.3 collective-permute-start.7
  78.9 22.8 %collective-permute-done.7.rest_2_ = f32[256,512]{1,0:T(8,128)S(1)} collective-permute-done((f32[256,512]{1,0:T(8,128)S(1)}, f32[256,512]{1,0:T(8,128)S(1)}, u32[]{:S(2)}, u32[]{:S(2)}) %collective-permute-start.7) | collective-permute-done | bytes 524320 | tf_op jit(solution)/shard_map/orthogonal/ppermute | solution.py:29
  101.8 0.8 slice.9
  102.5 2.0 %collective-permute-start.9 = (f32[128,512]{1,0:T(8,128)}, f32[128,512]{1,0:T(8,128)S(1)}, u32[]{:S(2)}, u32[]{:S(2)}) collective-permute-start(f32[128,512]{1,0:T(8,128)} %slice.9), channel_id=1, source_target_pairs={{0,6},{2,0},{4,2},{6,4},{1,7},{3,1},{5,3},{7,5},{8,14},{10,8},{12,... | collective-permute-start | bytes 786440 | tf_op jit(solution)/shard_map/orthogonal/ppermute | solution.py:29
  104.6 0.8 slice.8
  105.4 2.4 %collective-permute-start.10 = (f32[256,512]{1,0:T(8,128)S(1)}, f32[256,512]{1,0:T(8,128)S(1)}, u32[]{:S(2)}, u32[]{:S(2)}) collective-permute-start(f32[256,512]{1,0:T(8,128)S(1)} %constant_dynamic-update-slice_fusion.rest_0_), channel_id=1, source_target_pairs={{0,1},{1,0},{2,3},{3,2},{4,5},{5,4},{6,7},{7,6},{8,9},{9,8},{10,11... | collective-permute-start | bytes 1572872 | tf_op jit(solution)/shard_map/orthogonal/ppermute | solution.py:29
  108.9 2.6 %collective-permute-start.14 = (f32[128,512]{1,0:T(8,128)S(1)}, f32[128,512]{1,0:T(8,128)S(1)}, u32[]{:S(2)}, u32[]{:S(2)}) collective-permute-start(f32[128,512]{1,0:T(8,128)S(1)} %collective-permute-done.9.rest_4_), channel_id=1, source_target_pairs={{0,1},{1,0},{2,3},{3,2},{4,5},{5,4},{6,7},{7,6},{8,9},{9,8},{10,11... | collective-permute-start | bytes 786440 | tf_op jit(solution)/shard_map/orthogonal/ppermute | solution.py:29
  111.5 1.4 collective-permute-done.8.rest_3_
  112.9 2.8 %collective-permute-start.13 = (f32[128,512]{1,0:T(8,128)}, f32[128,512]{1,0:T(8,128)S(1)}, u32[]{:S(2)}, u32[]{:S(2)}) collective-permute-start(f32[128,512]{1,0:T(8,128)} %collective-permute-done.8.rest_3_), channel_id=1, source_target_pairs={{0,1},{1,0},{2,3},{3,2},{4,5},{5,4},{6,7},{7,6},{8,9},{9,8},{10,11... | collective-permute-start | bytes 786440 | tf_op jit(solution)/shard_map/orthogonal/ppermute | solution.py:29
  116.4 0.7 copy-done.9
  117.1 0.8 copy-done.10
  118.0 0.7 copy-done.5
  118.7 15.9 %solve.1 = f32[64,512]{1,0:T(8,128)} custom-call(s32[2,16]{1,0:T(2,128)} %blocks.1, s32[2]{0:T(128)} %counts.1, s32[8]{0:T(128)} %fusion.2.slots, f32[1536,512]{1,0:T(8,128)} %all-gather.6.cloned.1.call-done.own, f32[256,512]{1,0:T(8,128)} %copy-done.2, f32[256,512]{1,0:T(8,128)} %copy-done.1, f32[256,512]{1,0:T(8,128)} %copy-done, ...), custom_call_target="tpu_custom_call" | custom-call | flops 1610612736 | bytes 8388608 | tf_op jit(solution)/shard_map/solve/pallas_call | solution.py:33
  134.7 1.2 collective-permute-start.16
  136.9 0.8 collective-permute-start.18
  137.7 0.9 constant_dynamic-update-slice_fusion.9
  138.6 2.6 %collective-permute-done.17 = f32[64,512]{1,0:T(8,128)S(1)} collective-permute-done((f32[64,512]{1,0:T(8,128)}, f32[64,512]{1,0:T(8,128)S(1)}, u32[]{:S(2)}, u32[]{:S(2)}) %collective-permute-start.17) | collective-permute-done | bytes 131104 | tf_op jit(solution)/shard_map/share/ppermute | solution.py:29
  141.3 1.7 collective-permute-start.21
  143.0 1.6 collective-permute-done.15
  145.2 0.9 collective-permute-done.19
  146.2 1.0 copy-done.15
  147.2 6.9 %half_back.1 = (f32[512,256]{1,0:T(8,128)}, f32[512,128]{1,0:T(8,128)}, f32[512,128]{1,0:T(8,128)}) custom-call(s32[16,16]{1,0:T(8,128)} %bitcast.13, s32[16]{0:T(128)} %add.109.places, f32[512,512]{1,0:T(8,128)} %copy-done.15, bf16[1536,256]{1,0:T(8,128)(2,1)} %get-tuple-element.23.win_hi, bf16[1536,256]{1,0:T(8,128)(2,1)} %get-tuple-element.24.win_lo, ...), custom_call_target="tpu_custom_call" | custom-call | flops 1207959552 | bytes 6291456 | tf_op jit(solution)/shard_map/half_back/pallas_call | solution.py:33
  154.1 4.9 %collective-permute-start.23 = (f32[512,128]{1,0:T(8,128)}, f32[512,128]{1,0:T(8,128)S(1)}, u32[]{:S(2)}, u32[]{:S(2)}) collective-permute-start(f32[512,128]{1,0:T(8,128)} %get-tuple-element.33), channel_id=1, source_target_pairs={{0,248},{8,0},{16,8},{24,16},{32,24},{40,32},{48,40},{56,48},{64,5... | collective-permute-start | bytes 786440 | tf_op jit(solution)/shard_map/half_back/ppermute | solution.py:29
  159.0 6.4 %collective-permute-done.22.above = f32[512,128]{1,0:T(8,128)S(1)} collective-permute-done((f32[512,128]{1,0:T(8,128)}, f32[512,128]{1,0:T(8,128)S(1)}, u32[]{:S(2)}, u32[]{:S(2)}) %collective-permute-start.22) | collective-permute-done | bytes 262176 | tf_op jit(solution)/shard_map/half_back/ppermute | solution.py:29
  165.4 0.7 copy-done.12
  166.2 4.5 %density.2 = f32[8,96,128]{2,1,0:T(8,128)} custom-call(bf16[512,1536]{1,0:T(8,128)(2,1)} %get-tuple-element.19.root_hi, bf16[512,1536]{1,0:T(8,128)(2,1)} %get-tuple-element.20.root_lo, f32[512,128]{1,0:T(8,128)} %copy-done.12, f32[512,256]{1,0:T(8,128)} %get-tuple-element.32.own, f32[512,128]{1,0:T(8,128)} %copy-done.14, f32[512,256]{1,0:T(8,128)} %reshape.67.mask), custom_call_target="tpu_custom_call" | custom-call | flops 1207959552 | bytes 6291456 | tf_op jit(solution)/shard_map/density/pallas_call | solution.py:33
  170.7 13.2 %all_to_all.5.packed = f32[8,96,128]{2,1,0:T(8,128)} all-to-all(f32[8,96,128]{2,1,0:T(8,128)} %density.2), channel_id=1, replica_groups=mesh['rows'=32,'cols'=4,'space'=2] {'cols','space'}, dimensions={0} | all-to-all | bytes 786432 | tf_op jit(solution)/shard_map/density/all_to_all | solution.py:307
  183.9 1.9 density.3
  (79 shorter events, 4.7 us)
Async XLA Ops:
  7.2 37.3 %all-gather.4.cloned.1.call-start = ((), (), s32[]{:S(2)}) async-start(), calls=%async_computation.1 | async-start | bytes 3538944 | tf_op jit(solution)/shard_map/inputs/all_gather | solution.py:220
  7.9 110.0 %all-gather.6.cloned.1.call-start = ((), (), s32[]{:S(2)}) async-start(), calls=%async_computation.2 | async-start | bytes 3538944 | tf_op jit(solution)/shard_map/orthogonal/all_gather | solution.py:253
  9.3 12.3 %copy-start.16 = (s32[2,16]{1,0:T(2,128)S(1)}, s32[2,16]{1,0:T(2,128)}, u32[]{:S(2)}) copy-start(s32[2,16]{1,0:T(2,128)} %blocks.1) | copy-start | bytes 388
  10.3 24.6 %collective-permute-start.1 = (f32[512,128]{1,0:T(8,128)}, f32[512,128]{1,0:T(8,128)S(1)}, u32[]{:S(2)}, u32[]{:S(2)}) collective-permute-start(f32[512,128]{1,0:T(8,128)} %get-tuple-element.41), channel_id=1, source_target_pairs={{0,248},{8,0},{16,8},{24,16},{32,24},{40,32},{48,40},{56,48},{64,5... | collective-permute-start | bytes 786440 | tf_op jit(solution)/shard_map/inputs/ppermute | solution.py:29
  18.9 16.0 %collective-permute-start = (f32[512,128]{1,0:T(8,128)}, f32[512,128]{1,0:T(8,128)S(1)}, u32[]{:S(2)}, u32[]{:S(2)}) collective-permute-start(f32[512,128]{1,0:T(8,128)} %get-tuple-element.42), channel_id=1, source_target_pairs={{0,8},{8,16},{16,24},{24,32},{32,40},{40,48},{48,56},{56,64},{64,7... | collective-permute-start | bytes 786440 | tf_op jit(solution)/shard_map/inputs/ppermute | solution.py:29
  35.0 0.7 copy-start.7
  35.7 0.7 copy-start.8
  49.2 11.9 %collective-permute-start.2 = (f32[512,128]{1,0:T(8,128)}, f32[512,128]{1,0:T(8,128)S(1)}, u32[]{:S(2)}, u32[]{:S(2)}) collective-permute-start(f32[512,128]{1,0:T(8,128)} %get-tuple-element.25), channel_id=1, source_target_pairs={{0,8},{8,16},{16,24},{24,32},{32,40},{40,48},{48,56},{56,64},{64,7... | collective-permute-start | bytes 786440 | tf_op jit(solution)/shard_map/half_done/ppermute | solution.py:29
  50.5 10.6 %collective-permute-start.3 = (f32[512,128]{1,0:T(8,128)}, f32[512,128]{1,0:T(8,128)S(1)}, u32[]{:S(2)}, u32[]{:S(2)}) collective-permute-start(f32[512,128]{1,0:T(8,128)} %get-tuple-element.27), channel_id=1, source_target_pairs={{0,248},{8,0},{16,8},{24,16},{32,24},{40,32},{48,40},{56,48},{64,5... | collective-permute-start | bytes 786440 | tf_op jit(solution)/shard_map/half_done/ppermute | solution.py:29
  61.1 0.7 copy-start.11
  61.1 0.8 copy-start.13
  66.6 10.7 %collective-permute-start.4 = (f32[128,512]{1,0:T(8,128)}, f32[128,512]{1,0:T(8,128)S(1)}, u32[]{:S(2)}, u32[]{:S(2)}) collective-permute-start(f32[128,512]{1,0:T(8,128)} %get-tuple-element.29), channel_id=1, source_target_pairs={{0,8},{8,16},{16,24},{24,32},{32,40},{40,48},{48,56},{56,64},{64,7... | collective-permute-start | bytes 786440 | tf_op jit(solution)/shard_map/orthogonal/ppermute | solution.py:29
  66.7 10.6 %collective-permute-start.5 = (f32[128,512]{1,0:T(8,128)}, f32[128,512]{1,0:T(8,128)S(1)}, u32[]{:S(2)}, u32[]{:S(2)}) collective-permute-start(f32[128,512]{1,0:T(8,128)} %get-tuple-element.30), channel_id=1, source_target_pairs={{0,248},{8,0},{16,8},{24,16},{32,24},{40,32},{48,40},{56,48},{64,5... | collective-permute-start | bytes 786440 | tf_op jit(solution)/shard_map/orthogonal/ppermute | solution.py:29
  77.4 40.5 %copy-start.2 = (f32[256,512]{1,0:T(8,128)}, f32[256,512]{1,0:T(8,128)S(1)}, u32[]{:S(2)}) copy-start(f32[256,512]{1,0:T(8,128)S(1)} %constant_dynamic-update-slice_fusion.rest_0_) | copy-start | bytes 1572868
  77.4 24.4 %collective-permute-start.7 = (f32[256,512]{1,0:T(8,128)S(1)}, f32[256,512]{1,0:T(8,128)S(1)}, u32[]{:S(2)}, u32[]{:S(2)}) collective-permute-start(f32[256,512]{1,0:T(8,128)S(1)} %constant_dynamic-update-slice_fusion.rest_0_), channel_id=1, source_target_pairs={{0,6},{2,0},{4,2},{6,4},{1,7},{3,1},{5,3},{7,5},{8,14},{10,8},{12,... | collective-permute-start | bytes 1572872 | tf_op jit(solution)/shard_map/orthogonal/ppermute | solution.py:29
  78.7 25.9 %collective-permute-start.6 = (f32[256,512]{1,0:T(8,128)S(1)}, f32[256,512]{1,0:T(8,128)S(1)}, u32[]{:S(2)}, u32[]{:S(2)}) collective-permute-start(f32[256,512]{1,0:T(8,128)S(1)} %constant_dynamic-update-slice_fusion.rest_0_), channel_id=1, source_target_pairs={{0,2},{2,4},{4,6},{6,0},{1,3},{3,5},{5,7},{7,1},{8,10},{10,12},{12... | collective-permute-start | bytes 1572872 | tf_op jit(solution)/shard_map/orthogonal/ppermute | solution.py:29
  101.8 16.1 %copy-start = (f32[256,512]{1,0:T(8,128)}, f32[256,512]{1,0:T(8,128)S(1)}, u32[]{:S(2)}) copy-start(f32[256,512]{1,0:T(8,128)S(1)} %collective-permute-done.7.rest_2_) | copy-start | bytes 1572868
  102.5 6.4 %collective-permute-start.9 = (f32[128,512]{1,0:T(8,128)}, f32[128,512]{1,0:T(8,128)S(1)}, u32[]{:S(2)}, u32[]{:S(2)}) collective-permute-start(f32[128,512]{1,0:T(8,128)} %slice.9), channel_id=1, source_target_pairs={{0,6},{2,0},{4,2},{6,4},{1,7},{3,1},{5,3},{7,5},{8,14},{10,8},{12,... | collective-permute-start | bytes 786440 | tf_op jit(solution)/shard_map/orthogonal/ppermute | solution.py:29
  104.6 13.3 %copy-start.1 = (f32[256,512]{1,0:T(8,128)}, f32[256,512]{1,0:T(8,128)S(1)}, u32[]{:S(2)}) copy-start(f32[256,512]{1,0:T(8,128)S(1)} %collective-permute-done.6.rest_1_) | copy-start | bytes 1572868
  105.4 7.5 %collective-permute-start.8 = (f32[128,512]{1,0:T(8,128)}, f32[128,512]{1,0:T(8,128)}, u32[]{:S(2)}, u32[]{:S(2)}) collective-permute-start(f32[128,512]{1,0:T(8,128)} %slice.8), channel_id=1, source_target_pairs={{0,2},{2,4},{4,6},{6,0},{1,3},{3,5},{5,7},{7,1},{8,10},{10,12},{12... | collective-permute-start | bytes 786440 | tf_op jit(solution)/shard_map/orthogonal/ppermute | solution.py:29
  105.4 10.9 %collective-permute-start.10 = (f32[256,512]{1,0:T(8,128)S(1)}, f32[256,512]{1,0:T(8,128)S(1)}, u32[]{:S(2)}, u32[]{:S(2)}) collective-permute-start(f32[256,512]{1,0:T(8,128)S(1)} %constant_dynamic-update-slice_fusion.rest_0_), channel_id=1, source_target_pairs={{0,1},{1,0},{2,3},{3,2},{4,5},{5,4},{6,7},{7,6},{8,9},{9,8},{10,11... | collective-permute-start | bytes 1572872 | tf_op jit(solution)/shard_map/orthogonal/ppermute | solution.py:29
  107.8 8.6 %collective-permute-start.12 = (f32[256,512]{1,0:T(8,128)S(1)}, f32[256,512]{1,0:T(8,128)S(1)}, u32[]{:S(2)}, u32[]{:S(2)}) collective-permute-start(f32[256,512]{1,0:T(8,128)S(1)} %collective-permute-done.7.rest_2_), channel_id=1, source_target_pairs={{0,1},{1,0},{2,3},{3,2},{4,5},{5,4},{6,7},{7,6},{8,9},{9,8},{10,11... | collective-permute-start | bytes 1572872 | tf_op jit(solution)/shard_map/orthogonal/ppermute | solution.py:29
  107.8 10.1 %collective-permute-start.11 = (f32[256,512]{1,0:T(8,128)S(1)}, f32[256,512]{1,0:T(8,128)S(1)}, u32[]{:S(2)}, u32[]{:S(2)}) collective-permute-start(f32[256,512]{1,0:T(8,128)S(1)} %collective-permute-done.6.rest_1_), channel_id=1, source_target_pairs={{0,1},{1,0},{2,3},{3,2},{4,5},{5,4},{6,7},{7,6},{8,9},{9,8},{10,11... | collective-permute-start | bytes 1572872 | tf_op jit(solution)/shard_map/orthogonal/ppermute | solution.py:29
  108.9 9.0 %copy-start.6 = (f32[128,512]{1,0:T(8,128)}, f32[128,512]{1,0:T(8,128)S(1)}, u32[]{:S(2)}) copy-start(f32[128,512]{1,0:T(8,128)S(1)} %collective-permute-done.9.rest_4_) | copy-start | bytes 786436
  108.9 7.4 %collective-permute-start.14 = (f32[128,512]{1,0:T(8,128)S(1)}, f32[128,512]{1,0:T(8,128)S(1)}, u32[]{:S(2)}, u32[]{:S(2)}) collective-permute-start(f32[128,512]{1,0:T(8,128)S(1)} %collective-permute-done.9.rest_4_), channel_id=1, source_target_pairs={{0,1},{1,0},{2,3},{3,2},{4,5},{5,4},{6,7},{7,6},{8,9},{9,8},{10,11... | collective-permute-start | bytes 786440 | tf_op jit(solution)/shard_map/orthogonal/ppermute | solution.py:29
  112.9 4.2 %collective-permute-start.13 = (f32[128,512]{1,0:T(8,128)}, f32[128,512]{1,0:T(8,128)S(1)}, u32[]{:S(2)}, u32[]{:S(2)}) collective-permute-start(f32[128,512]{1,0:T(8,128)} %collective-permute-done.8.rest_3_), channel_id=1, source_target_pairs={{0,1},{1,0},{2,3},{3,2},{4,5},{5,4},{6,7},{7,6},{8,9},{9,8},{10,11... | collective-permute-start | bytes 786440 | tf_op jit(solution)/shard_map/orthogonal/ppermute | solution.py:29
  116.3 1.6 copy-start.3
  116.3 0.8 copy-start.9
  117.1 0.9 copy-start.4
  117.1 0.8 copy-start.10
  117.9 0.8 copy-start.5
  134.6 6.7 %collective-permute-start.17 = (f32[64,512]{1,0:T(8,128)}, f32[64,512]{1,0:T(8,128)S(1)}, u32[]{:S(2)}, u32[]{:S(2)}) collective-permute-start(f32[64,512]{1,0:T(8,128)} %solve.1), channel_id=1, source_target_pairs={{0,4},{2,6},{4,0},{6,2},{1,5},{3,7},{5,1},{7,3},{8,12},{10,14},{12... | collective-permute-start | bytes 393224 | tf_op jit(solution)/shard_map/share/ppermute | solution.py:29
  134.7 8.3 %collective-permute-start.16 = (f32[64,512]{1,0:T(8,128)}, f32[64,512]{1,0:T(8,128)S(1)}, u32[]{:S(2)}, u32[]{:S(2)}) collective-permute-start(f32[64,512]{1,0:T(8,128)} %solve.1), channel_id=1, source_target_pairs={{0,6},{2,0},{4,2},{6,4},{1,7},{3,1},{5,3},{7,5},{8,14},{10,8},{12,... | collective-permute-start | bytes 393224 | tf_op jit(solution)/shard_map/share/ppermute | solution.py:29
  135.9 8.8 %collective-permute-start.15 = (f32[64,512]{1,0:T(8,128)}, f32[64,512]{1,0:T(8,128)S(1)}, u32[]{:S(2)}, u32[]{:S(2)}) collective-permute-start(f32[64,512]{1,0:T(8,128)} %solve.1), channel_id=1, source_target_pairs={{0,2},{2,4},{4,6},{6,0},{1,3},{3,5},{5,7},{7,1},{8,10},{10,12},{12... | collective-permute-start | bytes 393224 | tf_op jit(solution)/shard_map/share/ppermute | solution.py:29
  136.9 8.3 %collective-permute-start.18 = (f32[64,512]{1,0:T(8,128)}, f32[64,512]{1,0:T(8,128)S(1)}, u32[]{:S(2)}, u32[]{:S(2)}) collective-permute-start(f32[64,512]{1,0:T(8,128)} %solve.1), channel_id=1, source_target_pairs={{0,1},{1,0},{2,3},{3,2},{4,5},{5,4},{6,7},{7,6},{8,9},{9,8},{10,11... | collective-permute-start | bytes 393224 | tf_op jit(solution)/shard_map/share/ppermute | solution.py:29
  141.3 4.9 %collective-permute-start.21 = (f32[64,512]{1,0:T(8,128)S(1)}, f32[64,512]{1,0:T(8,128)S(1)}, u32[]{:S(2)}, u32[]{:S(2)}) collective-permute-start(f32[64,512]{1,0:T(8,128)S(1)} %collective-permute-done.17), channel_id=1, source_target_pairs={{0,1},{1,0},{2,3},{3,2},{4,5},{5,4},{6,7},{7,6},{8,9},{9,8},{10,11... | collective-permute-start | bytes 393224 | tf_op jit(solution)/shard_map/share/ppermute | solution.py:29
  143.0 3.2 %collective-permute-start.20 = (f32[64,512]{1,0:T(8,128)S(1)}, f32[64,512]{1,0:T(8,128)S(1)}, u32[]{:S(2)}, u32[]{:S(2)}) collective-permute-start(f32[64,512]{1,0:T(8,128)S(1)} %collective-permute-done.16), channel_id=1, source_target_pairs={{0,1},{1,0},{2,3},{3,2},{4,5},{5,4},{6,7},{7,6},{8,9},{9,8},{10,11... | collective-permute-start | bytes 393224 | tf_op jit(solution)/shard_map/share/ppermute | solution.py:29
  144.6 1.5 collective-permute-start.19
  146.2 1.0 copy-start.15
  154.1 11.3 %collective-permute-start.22 = (f32[512,128]{1,0:T(8,128)}, f32[512,128]{1,0:T(8,128)S(1)}, u32[]{:S(2)}, u32[]{:S(2)}) collective-permute-start(f32[512,128]{1,0:T(8,128)} %get-tuple-element.31), channel_id=1, source_target_pairs={{0,8},{8,16},{16,24},{24,32},{32,40},{40,48},{48,56},{56,64},{64,7... | collective-permute-start | bytes 786440 | tf_op jit(solution)/shard_map/half_back/ppermute | solution.py:29
  154.1 11.3 %collective-permute-start.23 = (f32[512,128]{1,0:T(8,128)}, f32[512,128]{1,0:T(8,128)S(1)}, u32[]{:S(2)}, u32[]{:S(2)}) collective-permute-start(f32[512,128]{1,0:T(8,128)} %get-tuple-element.33), channel_id=1, source_target_pairs={{0,248},{8,0},{16,8},{24,16},{32,24},{40,32},{48,40},{56,48},{64,5... | collective-permute-start | bytes 786440 | tf_op jit(solution)/shard_map/half_back/ppermute | solution.py:29
  165.4 0.7 copy-start.12
  165.4 0.8 copy-start.14
Sparse Core Ops, SparseCore 0:
  9.8 34.5 all-gather.3
  66.7 38.9 all-gather.5

commit v3 on v2

--- a/solution.py
+++ b/solution.py
@@ -13,14 +13,12 @@
 CHUNK = 64
 LANES = 256
 ORDER = MAXB * BLK
-OWN_ROWS = 3 * SLAB
 NEAR = 4 * CHUNK
 f32 = jnp.float32
 bf16 = jnp.bfloat16
 ALL = ("cols", "space")
 VMEM = pl.BlockSpec(memory_space=pltpu.VMEM)
 SMEM = pl.BlockSpec(memory_space=pltpu.SMEM)
-PARAMS = pltpu.CompilerParams(vmem_limit_bytes=56 * 1024 * 1024)
 
 
 def passed_along(value, axis, steps):
@@ -29,14 +27,14 @@
     return lax.ppermute(value, axis, pairs)
 
 
-def kernel_call(body, shapes, operands, in_specs, scratch=(), flops=0, moved=0):
+def kernel_call(body, shapes, operands, in_specs, scratch=(), limit=12, flops=0, moved=0):
     return pl.pallas_call(
         body,
         out_shape=shapes,
         in_specs=in_specs,
         out_specs=jax.tree.map(lambda _: VMEM, shapes),
         scratch_shapes=list(scratch),
-        compiler_params=PARAMS,
+        compiler_params=pltpu.CompilerParams(vmem_limit_bytes=limit << 20),
         cost_estimate=pl.CostEstimate(flops=flops, bytes_accessed=moved, transcendentals=0),
     )(*operands)
 
@@ -107,81 +105,84 @@
         packed[c, CHUNK:, :] = jnp.where(lane < CHUNK, last[:half], pltpu.roll(last[half:], CHUNK, 1))
 
 
-def solve_kernel(blocks, counts, slots, own, *rest):
-    near, (out, gathered, assembled, sems) = rest[:-4], rest[-4:]
-    copies = [pltpu.make_async_copy(own, gathered.at[pl.ds(0, OWN_ROWS)], sems.at[0])]
-    at = OWN_ROWS
-    for n, piece in enumerate(near):
-        target = gathered.at[pl.ds(at, piece.shape[0])]
-        copies.append(pltpu.make_async_copy(piece, target, sems.at[n + 1]))
-        at += piece.shape[0]
-    for copy in copies:
-        copy.start()
-    for copy in copies:
-        copy.wait()
-    lane_block = lax.broadcasted_iota(jnp.int32, (BLK, 128), 1) // BLK
+def solve_kernel(blocks, counts, slots, whole, near, out, rows, turned, assembled):
     row_id = lax.broadcasted_iota(jnp.int32, (BLK, ORDER), 0)
     col_id = lax.broadcasted_iota(jnp.int32, (BLK, ORDER), 1)
+    dot = functools.partial(jnp.dot, preferred_element_type=f32)
+
+    def gather(g):
+        def one_row(k, carry):
+            q = blocks[g, k]
+            j, c = q // 16, (q % 16) // 2
+            base = (q % 2) * BLK + j * CHUNK
+            away = slots[c] * NEAR + base
+            there = pl.ds(pl.multiple_of(k * BLK, BLK), BLK)
+            sources = ((near, away), (whole, c * 3 * CHUNK + base), (near, away + CHUNK))
+            for panel, (source, start) in enumerate(sources):
+                keep = (k < counts[g]) & (jnp.abs(j - panel) <= 1)
+                block = source[pl.ds(pl.multiple_of(start, BLK), BLK), :]
+                rows[there, panel * SLAB : (panel + 1) * SLAB] = jnp.where(keep, block, 0.0)
+            return carry
+
+        def one_column(k, carry):
+            source = pl.ds(pl.multiple_of(blocks[g, k] * BLK, BLK), BLK)
+            there = pl.ds(pl.multiple_of(k * BLK, BLK), BLK)
+            assembled[g, there, :] = jnp.where(k < counts[g], turned[source, :], 0.0)
+            return carry
+
+        lax.fori_loop(0, MAXB, one_row, 0, unroll=4)
+        for panel in range(3):
+            cut = slice(panel * SLAB, (panel + 1) * SLAB)
+            turned[cut, :] = rows[:, cut].T
+        lax.fori_loop(0, MAXB, one_column, 0, unroll=4)
+
+    def scaled(g):
+        whole_block = assembled[g]
+        symmetric = 0.5 * (whole_block + whole_block.T)
+        squares = jnp.sum(symmetric * symmetric, keepdims=True) + 1e-06
+        size = jnp.full((1, 1), counts[g] * BLK, jnp.int32).astype(f32)
+        return symmetric * (jnp.sqrt(size) / (2.0 * jnp.sqrt(squares)))
+
+    def step(iterate):
+        parts = split(iterate)
+        return 1.5 * iterate - 0.5 * dot3(parts, split(dot3(parts, parts)))
+
+    def thin(home, parts):
+        high, low = split(home)
+        both = dot(jnp.concatenate([high, low], axis=0), parts[0])
+        return both[:BLK] + both[BLK:] + dot(high, parts[1])
+
     for g in range(2):
-        live = counts[g]
-        spots = []
-        for i in range(MAXB):
-            p = blocks[g, i]
-            panel = p // 16
-            tile = pl.multiple_of(((p % 16) // 4) * 128, 128)
-            shift = lax.rem((i % 4 - p % 4) * BLK + 128, 128)
-            spots.append((panel, tile, shift, i < live))
-
-        def gather_row(k, carry):
-            q = blocks[g, k]
-            j = q // 16
-            c = (q % 16) // 2
-            base = (q % 2) * BLK + j * CHUNK
-            away = OWN_ROWS + slots[c] * NEAR + base
-            starts = (away, c * 3 * CHUNK + base, away + CHUNK)
-            row_live = k < live
-            for t in range(4):
-                total = jnp.zeros((BLK, 128), f32)
-                for ii in range(4):
-                    panel, tile, shift, col_live = spots[t * 4 + ii]
-                    start = jnp.where(panel == 0, starts[0], jnp.where(panel == 1, starts[1], starts[2]))
-                    start = pl.multiple_of(start, BLK)
-                    here = row_live & col_live & (jnp.abs(panel - j) <= 1)
-                    block = pltpu.roll(gathered[pl.ds(start, BLK), pl.ds(tile, 128)], shift, 1)
-                    total = jnp.where(lane_block == jnp.where(here, ii, 9), block, total)
-                assembled[pl.ds(pl.multiple_of(k * BLK, BLK), BLK), t * 128 : (t + 1) * 128] = total
-            return carry
-
-        lax.fori_loop(0, MAXB, gather_row, 0)
-        whole = assembled[...]
-        symmetric = 0.5 * (whole + whole.T)
-        squares = jnp.sum(symmetric * symmetric, keepdims=True) + 1e-06
-        size = jnp.full((1, 1), live * BLK, jnp.int32).astype(f32)
-        iterate = symmetric * (jnp.sqrt(size) / (2.0 * jnp.sqrt(squares)))
-        parts = split(iterate)
-        square = split(dot3(parts, parts))
-        iterate = 1.5 * iterate - 0.5 * dot3(parts, square)
+        gather(g)
+    iterates = [step(iterate) for iterate in [scaled(g) for g in range(2)]]
+    for g, iterate in enumerate(iterates):
         parts = split(iterate)
         home = iterate[:BLK]
-        once = dot3((parts[0][:BLK], parts[1][:BLK]), parts)
-        home = 1.5 * home - 0.5 * dot3(split(once), parts)
+        home = 1.5 * home - 0.5 * thin(thin(home, parts), parts)
         out[g * BLK : (g + 1) * BLK, :] = 0.5 * (jnp.where(row_id == col_id, 1.0, 0.0) - home)
 
 
 def back_kernel(blocks, places, rows, win_hi, win_lo, mask, own, up, down, full, part_hi, part_lo):
-    def one_block(e, carry):
-        g = places[e]
-        for i in range(MAXB):
-            source = pl.ds(pl.multiple_of(blocks[g, i] * BLK, BLK), BLK)
-            target = slice(i * BLK, (i + 1) * BLK)
-            part_hi[target, :] = win_hi[source, :]
-            part_lo[target, :] = win_lo[source, :]
-        home = split(rows[pl.ds(pl.multiple_of(e * BLK, BLK), BLK), :])
-        there = pl.ds(pl.multiple_of(g * BLK, BLK), BLK)
-        full[there, :] = dot3(home, (part_hi[...], part_lo[...])) * mask[there, :]
+    dot = functools.partial(jnp.dot, preferred_element_type=f32)
+    width = part_hi.shape[0]
+
+    def some_blocks(step, carry):
+        for slot in range(width):
+            e = step * width + slot
+            g = places[e]
+            for i in range(MAXB):
+                source = pl.ds(pl.multiple_of(blocks[g, i] * BLK, BLK), BLK)
+                target = slice(i * BLK, (i + 1) * BLK)
+                part_hi[slot, target, :] = win_hi[source, :]
+                part_lo[slot, target, :] = win_lo[source, :]
+            high, low = split(rows[pl.ds(pl.multiple_of(e * BLK, BLK), BLK), :])
+            both = dot(jnp.concatenate([high, low], axis=0), part_hi[slot])
+            there = pl.ds(pl.multiple_of(g * BLK, BLK), BLK)
+            total = both[:BLK] + both[BLK:] + dot(high, part_lo[slot])
+            full[there, :] = total * mask[there, :]
         return carry
 
-    lax.fori_loop(0, SLAB // BLK, one_block, 0)
+    lax.fori_loop(0, SLAB // BLK // width, some_blocks, 0)
     send_parts(full[...], own, up, down)
 
 
@@ -257,6 +258,7 @@
         opposite = (passed_along(before[:half], "cols", 1), passed_along(after[half:], "cols", -1))
         near = (near, before, after) + opposite
         near = near + tuple(passed_along(piece, "space", 1) for piece in near)
+        near = jnp.concatenate(near, axis=0)
         steps = jnp.arange(SLAB // CHUNK)
         turn = lax.rem(steps // 2 - col + 4, 4)
         slots = jnp.where(turn == 3, 1, jnp.where(turn == 0, 0, turn + 1))
@@ -265,13 +267,14 @@
         rows = kernel_call(
             solve_kernel,
             sds((2 * BLK, ORDER), f32),
-            (sub_blocks, sub_count, slots, whole) + near,
-            [SMEM] * 3 + [pl.BlockSpec(memory_space=pl.ANY)] * 11,
+            (sub_blocks, sub_count, slots, whole, near),
+            [SMEM] * 3 + [VMEM] * 2,
             scratch=[
-                pltpu.VMEM((OWN_ROWS + 8 * NEAR, SLAB), f32),
-                pltpu.VMEM((ORDER, ORDER), f32),
-                pltpu.SemaphoreType.DMA((11,)),
+                pltpu.VMEM((ORDER, 3 * SLAB), f32),
+                pltpu.VMEM((3 * SLAB, ORDER), f32),
+                pltpu.VMEM((2, ORDER, ORDER), f32),
             ],
+            limit=24,
             flops=12 * ORDER**3,
             moved=8 << 20,
         )
@@ -290,8 +293,8 @@
             [SMEM, SMEM] + [VMEM] * 4,
             scratch=[
                 pltpu.VMEM((SLAB, LANES), f32),
-                pltpu.VMEM((ORDER, LANES), bf16),
-                pltpu.VMEM((ORDER, LANES), bf16),
+                pltpu.VMEM((4, ORDER, LANES), bf16),
+                pltpu.VMEM((4, ORDER, LANES), bf16),
             ],
             **product,
         )

time: 193 us -> 180 us (0.933)
  Pallas kernels: 44.1 us -> 21.1 us
  local copies, waits for them, and re-layouts: 12.7 us -> 23.6 us
  waiting for transfers between devices: 52.4 us -> 47.4 us
  starting transfers between devices: 40 us -> 44.9 us
    pallas_call x7, Pallas kernels: 44.1 us -> 21.1 us  [kernel_call(): pl.pallas_call(body, out_shape=shapes, in_specs=in_specs, out_specs=jax.t...]
    unnamed x43, local copies, waits for them, and re-layouts: 7.34 us -> 18.7 us
    ppermute x24, waiting for transfers between devices: 48.9 us -> 41.4 us  [passed_along(): return lax.ppermute(value, axis, pairs)]
    ppermute x24, starting transfers between devices: 40 us -> 44.8 us  [passed_along(): return lax.ppermute(value, axis, pairs)]
    all_gather x1, waiting for transfers between devices: 2.74 us -> 5.34 us  [shards(): ham = lax.all_gather(hamiltonian, ALL, axis=0, tiled=True)]
  transfers between devices with their start and end apart: 26 -> 26, of which waited for: 10 -> 9; matrix products, arithmetic and copies ran while one was open for 5% -> 9% of each run, Pallas kernels for 3% -> 1%
where the time goes in v3:
time: 180 us; the launch traced here: 179 us
  waiting for transfers between devices  47.4 us (26%)
  starting transfers between devices  44.9 us (25%)
  blocking collectives  24.4 us (14%)
  local copies, waits for them, and re-layouts  23.6 us (13%)
  Pallas kernels  21.1 us (12%)
  between operations  14.3 us (8%)
  other arithmetic  3.31 us (2%)
    ppermute x24, starting transfers between devices, passed_along(): return lax.ppermute(value, axis, pairs)  44.8 us
    ppermute x24, waiting for transfers between devices, passed_along(): return lax.ppermute(value, axis, pairs)  41.4 us
    pallas_call x7, Pallas kernels, kernel_call(): pl.pallas_call(body, out_shape=shapes, in_specs=in_specs, out_specs=jax.t...  21.1 us
    unnamed x43, local copies, waits for them, and re-layouts  18.7 us
    all_to_all x1, blocking collectives, shards(): packed = lax.all_to_all(packed, ALL, 0, 0)  12.8 us
    all_gather x1, blocking collectives, shards(): lists = lax.all_gather(sub_blocks, ALL, axis=0, tiled=True)  11.6 us
    all_gather x1, waiting for transfers between devices, shards(): ham = lax.all_gather(hamiltonian, ALL, axis=0, tiled=True)  5.34 us
  transfers between devices with their start and end apart: 26, of which 9 were waited for; matrix products, arithmetic and copies ran while one was open for 9% of the time, Pallas kernels for 1%

profile of v3, /device:TPU:1, one launch (start us, length us, event | category | flops | bytes accessed | tf_op | source)
XLA Modules:
  0.0 179.0 jit_solution(1146476020909709924)
XLA Ops:
  8.0 1.4 constant_dynamic-slice_fusion.1
  9.4 1.0 pad_maximum_fusion.1
  10.4 2.5 %collective-permute-start = (f32[512,128]{1,0:T(8,128)}, f32[512,128]{1,0:T(8,128)S(1)}, u32[]{:S(2)}, u32[]{:S(2)}) collective-permute-start(f32[512,128]{1,0:T(8,128)} %get-tuple-element.46), channel_id=1, source_target_pairs={{0,8},{8,16},{16,24},{24,32},{32,40},{40,48},{48,56},{56,64},{64,7... | collective-permute-start | bytes 786440 | tf_op jit(solution)/shard_map/inputs/ppermute | solution.py:27
  12.8 6.1 %collective-permute-start.1 = (f32[512,128]{1,0:T(8,128)}, f32[512,128]{1,0:T(8,128)S(1)}, u32[]{:S(2)}, u32[]{:S(2)}) collective-permute-start(f32[512,128]{1,0:T(8,128)} %get-tuple-element.45), channel_id=1, source_target_pairs={{0,248},{8,0},{16,8},{24,16},{32,24},{40,32},{48,40},{56,48},{64,5... | collective-permute-start | bytes 786440 | tf_op jit(solution)/shard_map/inputs/ppermute | solution.py:27
  20.8 11.6 %all-gather = s32[8,2,16]{2,1,0:T(2,128)S(1)} all-gather(s32[1,2,16]{2,1,0:T(2,128)S(1)} %bitcast.13), channel_id=1, replica_groups=mesh['rows'=32,'cols'=4,'space'=2] {'cols','space'}, dimensions={0}, use_global_device_ids=true | all-gather | bytes 1152 | tf_op jit(solution)/shard_map/inputs/all_gather | solution.py:238
  32.4 1.3 maximum_maximum_fusion.own
  33.7 1.9 %copy-done.3 = f32[512,1536]{1,0:T(8,128)S(1)} copy-done((f32[512,1536]{1,0:T(8,128)S(1)}, f32[512,1536]{1,0:T(8,128)}, u32[]{:S(2)}) %copy-start.3) | copy-done | bytes 3145752
  35.6 1.4 inputs.1
  37.0 1.2 copy-done
  38.2 0.9 copy-done.6
  39.1 5.3 %all-gather.4.cloned.1.call-done.ham = f32[512,1536]{1,0:T(8,128)} async-done(((f32[64,1536]{1,0:T(8,128)}), f32[512,1536]{1,0:T(8,128)}) %all-gather.4.cloned.1.call-update) | async-done | bytes 3145744 | tf_op jit(solution)/shard_map/inputs/all_gather | solution.py:221
  44.4 2.0 %copy-done.5 = f32[512,1536]{1,0:T(8,128)S(1)} copy-done((f32[512,1536]{1,0:T(8,128)S(1)}, f32[512,1536]{1,0:T(8,128)}, u32[]{:S(2)}) %copy-start.5) | copy-done | bytes 3145752
  46.4 1.1 copy-done.7
  47.6 1.5 half_done.1
  49.1 1.3 collective-permute-start.2
  50.4 4.0 %collective-permute-start.3 = (f32[512,128]{1,0:T(8,128)S(1)}, f32[512,128]{1,0:T(8,128)S(1)}, u32[]{:S(2)}, u32[]{:S(2)}) collective-permute-start(f32[512,128]{1,0:T(8,128)S(1)} %get-tuple-element.27), channel_id=1, source_target_pairs={{0,248},{8,0},{16,8},{24,16},{32,24},{40,32},{48,40},{56,48},{64,5... | collective-permute-start | bytes 786440 | tf_op jit(solution)/shard_map/half_done/ppermute | solution.py:27
  54.4 6.4 %collective-permute-done.2.above = f32[512,128]{1,0:T(8,128)S(1)} collective-permute-done((f32[512,128]{1,0:T(8,128)S(1)}, f32[512,128]{1,0:T(8,128)S(1)}, u32[]{:S(2)}, u32[]{:S(2)}) %collective-permute-start.2) | collective-permute-done | bytes 262176 | tf_op jit(solution)/shard_map/half_done/ppermute | solution.py:27
  60.8 2.3 %orthogonal.1 = (f32[192,512]{1,0:T(8,128)}, f32[128,512]{1,0:T(8,128)S(1)}, f32[128,512]{1,0:T(8,128)S(1)}) custom-call(bf16[512,1536]{1,0:T(8,128)(2,1)S(1)} %get-tuple-element.19.root_hi, bf16[512,1536]{1,0:T(8,128)(2,1)S(1)} %copy-done.1, f32[512,128]{1,0:T(8,128)S(1)} %collective-permute-done.2.above, f32[512,256]{1,0:T(8,128)S(1)} %get-tuple-element.26.own, ...), custom_call_target="tpu_custom_call" | custom-call | flops 1207959552 | bytes 6291456 | tf_op jit(solution)/shard_map/orthogonal/pallas_call | solution.py:31
  63.2 4.8 %collective-permute-start.5 = (f32[128,512]{1,0:T(8,128)S(1)}, f32[128,512]{1,0:T(8,128)S(1)}, u32[]{:S(2)}, u32[]{:S(2)}) collective-permute-start(f32[128,512]{1,0:T(8,128)S(1)} %get-tuple-element.30), channel_id=1, source_target_pairs={{0,248},{8,0},{16,8},{24,16},{32,24},{40,32},{48,40},{56,48},{64,5... | collective-permute-start | bytes 786440 | tf_op jit(solution)/shard_map/orthogonal/ppermute | solution.py:27
  68.0 5.6 %collective-permute-done.4 = f32[128,512]{1,0:T(8,128)S(1)} collective-permute-done((f32[128,512]{1,0:T(8,128)S(1)}, f32[128,512]{1,0:T(8,128)S(1)}, u32[]{:S(2)}, u32[]{:S(2)}) %collective-permute-start.4) | collective-permute-done | bytes 262176 | tf_op jit(solution)/shard_map/orthogonal/ppermute | solution.py:27
  73.6 0.9 constant_dynamic-update-slice_fusion.1
  74.5 0.9 constant_dynamic-update-slice_fusion
  75.5 2.6 %collective-permute-start.7 = (f32[256,512]{1,0:T(8,128)}, f32[256,512]{1,0:T(8,128)S(1)}, u32[]{:S(2)}, u32[]{:S(2)}) collective-permute-start(f32[256,512]{1,0:T(8,128)} %get-tuple-element.41), channel_id=1, source_target_pairs={{0,6},{2,0},{4,2},{6,4},{1,7},{3,1},{5,3},{7,5},{8,14},{10,8},{12,... | collective-permute-start | bytes 1572872 | tf_op jit(solution)/shard_map/orthogonal/ppermute | solution.py:27
  78.1 2.4 %collective-permute-start.10 = (f32[256,512]{1,0:T(8,128)}, f32[256,512]{1,0:T(8,128)S(1)}, u32[]{:S(2)}, u32[]{:S(2)}) collective-permute-start(f32[256,512]{1,0:T(8,128)} %get-tuple-element.41), channel_id=1, source_target_pairs={{0,1},{1,0},{2,3},{3,2},{4,5},{5,4},{6,7},{7,6},{8,9},{9,8},{10,11... | collective-permute-start | bytes 1572872 | tf_op jit(solution)/shard_map/orthogonal/ppermute | solution.py:27
  80.6 20.2 %collective-permute-done.6 = f32[256,512]{1,0:T(8,128)} collective-permute-done((f32[256,512]{1,0:T(8,128)}, f32[256,512]{1,0:T(8,128)}, u32[]{:S(2)}, u32[]{:S(2)}) %collective-permute-start.6) | collective-permute-done | bytes 524320 | tf_op jit(solution)/shard_map/orthogonal/ppermute | solution.py:27
  100.8 1.0 slice.8
  101.9 2.7 %collective-permute-start.9 = (f32[128,512]{1,0:T(8,128)S(1)}, f32[128,512]{1,0:T(8,128)S(1)}, u32[]{:S(2)}, u32[]{:S(2)}) collective-permute-start(f32[128,512]{1,0:T(8,128)S(1)} %slice.9), channel_id=1, source_target_pairs={{0,6},{2,0},{4,2},{6,4},{1,7},{3,1},{5,3},{7,5},{8,14},{10,8},{12,... | collective-permute-start | bytes 786440 | tf_op jit(solution)/shard_map/orthogonal/ppermute | solution.py:27
  104.7 1.7 collective-permute-start.11
  106.5 1.9 %constant_dynamic-update-slice_fusion.10 = f32[2048,512]{1,0:T(8,128)} fusion(f32[2048,512]{1,0:T(8,128)} %get-tuple-element.42, f32[256,512]{1,0:T(8,128)} %collective-permute-done.6), kind=kLoop, calls=%fused_computation.13 | loop fusion | bytes 1048576
  108.4 0.9 constant_dynamic-update-slice_fusion.9
  109.7 2.0 %collective-permute-start.13 = (f32[128,512]{1,0:T(8,128)S(1)}, f32[128,512]{1,0:T(8,128)S(1)}, u32[]{:S(2)}, u32[]{:S(2)}) collective-permute-start(f32[128,512]{1,0:T(8,128)S(1)} %collective-permute-done.8), channel_id=1, source_target_pairs={{0,1},{1,0},{2,3},{3,2},{4,5},{5,4},{6,7},{7,6},{8,9},{9,8},{10,11... | collective-permute-start | bytes 786440 | tf_op jit(solution)/shard_map/orthogonal/ppermute | solution.py:27
  113.2 0.8 constant_dynamic-update-slice_fusion.6
  117.2 1.9 %copy-done.4 = f32[1536,512]{1,0:T(8,128)S(1)} copy-done((f32[1536,512]{1,0:T(8,128)S(1)}, f32[1536,512]{1,0:T(8,128)}, u32[]{:S(2)}) %copy-start.4) | copy-done | bytes 3145752
  119.1 10.7 %solve.1 = f32[64,512]{1,0:T(8,128)S(1)} custom-call(s32[2,16]{1,0:T(2,128)S(1)} %copy-done.9, s32[2]{0:T(128)S(1)} %copy-done.10, s32[8]{0:T(128)S(1)} %fusion.2.slots, f32[1536,512]{1,0:T(8,128)S(1)} %copy-done.4, f32[2048,512]{1,0:T(8,128)} %constant_dynamic-update-slice_fusion.2.near), custom_call_target="tpu_custom_call" | custom-call | flops 1610612736 | bytes 8388608 | tf_op jit(solution)/shard_map/solve/pallas_call | solution.py:31
  130.0 2.8 %collective-permute-start.16 = (f32[64,512]{1,0:T(8,128)S(1)}, f32[64,512]{1,0:T(8,128)S(1)}, u32[]{:S(2)}, u32[]{:S(2)}) collective-permute-start(f32[64,512]{1,0:T(8,128)S(1)} %solve.1), channel_id=1, source_target_pairs={{0,6},{2,0},{4,2},{6,4},{1,7},{3,1},{5,3},{7,5},{8,14},{10,8},{12,... | collective-permute-start | bytes 393224 | tf_op jit(solution)/shard_map/share/ppermute | solution.py:27
  132.9 1.3 collective-permute-start.17
  134.7 1.1 collective-permute-done.15
  135.8 1.2 collective-permute-start.19
  137.1 2.3 %collective-permute-start.20 = (f32[64,512]{1,0:T(8,128)S(1)}, f32[64,512]{1,0:T(8,128)S(1)}, u32[]{:S(2)}, u32[]{:S(2)}) collective-permute-start(f32[64,512]{1,0:T(8,128)S(1)} %collective-permute-done.16), channel_id=1, source_target_pairs={{0,1},{1,0},{2,3},{3,2},{4,5},{5,4},{6,7},{7,6},{8,9},{9,8},{10,11... | collective-permute-start | bytes 393224 | tf_op jit(solution)/shard_map/share/ppermute | solution.py:27
  139.9 1.2 collective-permute-start.21
  141.2 0.9 collective-permute-done.21
  142.1 1.1 copy-done.8
  143.2 2.8 %half_back.1 = (f32[512,256]{1,0:T(8,128)S(1)}, f32[512,128]{1,0:T(8,128)S(1)}, f32[512,128]{1,0:T(8,128)S(1)}) custom-call(s32[16,16]{1,0:T(8,128)S(1)} %bitcast.12, s32[16]{0:T(128)S(1)} %add.109.places, f32[512,512]{1,0:T(8,128)S(1)} %constant_dynamic-update-slice_fusion.13.rows, bf16[1536,256]{1,0:T(8,128)(2,1)S(1)} %get-tuple-element.23.win_hi, ...), custom_call_target="tpu_custom_call" | custom-call | flops 1207959552 | bytes 6291456 | tf_op jit(solution)/shard_map/half_back/pallas_call | solution.py:31
  146.1 4.8 %collective-permute-start.23 = (f32[512,128]{1,0:T(8,128)S(1)}, f32[512,128]{1,0:T(8,128)S(1)}, u32[]{:S(2)}, u32[]{:S(2)}) collective-permute-start(f32[512,128]{1,0:T(8,128)S(1)} %get-tuple-element.33), channel_id=1, source_target_pairs={{0,248},{8,0},{16,8},{24,16},{32,24},{40,32},{48,40},{56,48},{64,5... | collective-permute-start | bytes 786440 | tf_op jit(solution)/shard_map/half_back/ppermute | solution.py:27
  150.9 6.1 %collective-permute-done.22.above = f32[512,128]{1,0:T(8,128)S(1)} collective-permute-done((f32[512,128]{1,0:T(8,128)S(1)}, f32[512,128]{1,0:T(8,128)S(1)}, u32[]{:S(2)}, u32[]{:S(2)}) %collective-permute-start.22) | collective-permute-done | bytes 262176 | tf_op jit(solution)/shard_map/half_back/ppermute | solution.py:27
  156.9 1.5 density.2
  158.5 12.8 %all_to_all.5.packed = f32[8,96,128]{2,1,0:T(8,128)S(1)} all-to-all(f32[8,96,128]{2,1,0:T(8,128)S(1)} %density.2), channel_id=1, replica_groups=mesh['rows'=32,'cols'=4,'space'=2] {'cols','space'}, dimensions={0} | all-to-all | bytes 786432 | tf_op jit(solution)/shard_map/density/all_to_all | solution.py:310
  171.3 0.9 density.3
  (80 shorter events, 9.7 us)
Async XLA Ops:
  7.2 13.6 %copy-start.9 = (s32[2,16]{1,0:T(2,128)S(1)}, s32[2,16]{1,0:T(2,128)}, u32[]{:S(2)}) copy-start(s32[2,16]{1,0:T(2,128)} %blocks.1) | copy-start | bytes 388
  7.2 37.3 %all-gather.4.cloned.1.call-start = ((), (), s32[]{:S(2)}) async-start(), calls=%async_computation.1 | async-start | bytes 3538944 | tf_op jit(solution)/shard_map/inputs/all_gather | solution.py:221
  7.9 109.3 %all-gather.6.cloned.1.call-start = ((), (), s32[]{:S(2)}) async-start(), calls=%async_computation.2 | async-start | bytes 3538944 | tf_op jit(solution)/shard_map/orthogonal/all_gather | solution.py:254
  9.4 10.6 %copy-start.11 = (f32[512,64]{1,0:T(8,128)}, f32[512,64]{1,0:T(8,128)S(1)}, u32[]{:S(2)}) copy-start(f32[512,64]{1,0:T(8,128)S(1)} %get-tuple-element.39) | copy-start | bytes 393220
  9.4 10.5 %copy-start.12 = (f32[512,64]{1,0:T(8,128)}, f32[512,64]{1,0:T(8,128)S(1)}, u32[]{:S(2)}) copy-start(f32[512,64]{1,0:T(8,128)S(1)} %get-tuple-element.40) | copy-start | bytes 393220
  10.4 23.3 %collective-permute-start = (f32[512,128]{1,0:T(8,128)}, f32[512,128]{1,0:T(8,128)S(1)}, u32[]{:S(2)}, u32[]{:S(2)}) collective-permute-start(f32[512,128]{1,0:T(8,128)} %get-tuple-element.46), channel_id=1, source_target_pairs={{0,8},{8,16},{16,24},{24,32},{32,40},{40,48},{48,56},{56,64},{64,7... | collective-permute-start | bytes 786440 | tf_op jit(solution)/shard_map/inputs/ppermute | solution.py:27
  12.8 20.8 %collective-permute-start.1 = (f32[512,128]{1,0:T(8,128)}, f32[512,128]{1,0:T(8,128)S(1)}, u32[]{:S(2)}, u32[]{:S(2)}) collective-permute-start(f32[512,128]{1,0:T(8,128)} %get-tuple-element.45), channel_id=1, source_target_pairs={{0,248},{8,0},{16,8},{24,16},{32,24},{40,32},{48,40},{56,48},{64,5... | collective-permute-start | bytes 786440 | tf_op jit(solution)/shard_map/inputs/ppermute | solution.py:27
  33.6 2.0 %copy-start.3 = (f32[512,1536]{1,0:T(8,128)S(1)}, f32[512,1536]{1,0:T(8,128)}, u32[]{:S(2)}) copy-start(f32[512,1536]{1,0:T(8,128)} %root.1) | copy-start | bytes 9437188
  37.0 1.3 copy-start
  38.2 0.9 copy-start.6
  44.4 16.4 %copy-start.1 = (bf16[512,1536]{1,0:T(8,128)(2,1)S(1)}, bf16[512,1536]{1,0:T(8,128)(2,1)}, u32[]{:S(2)}) copy-start(bf16[512,1536]{1,0:T(8,128)(2,1)} %copy-done) | copy-start | bytes 4718596
  44.4 2.0 %copy-start.5 = (f32[512,1536]{1,0:T(8,128)S(1)}, f32[512,1536]{1,0:T(8,128)}, u32[]{:S(2)}) copy-start(f32[512,1536]{1,0:T(8,128)} %all-gather.4.cloned.1.call-done.ham) | copy-start | bytes 9437188
  46.4 1.1 copy-start.7
  49.1 11.7 %collective-permute-start.2 = (f32[512,128]{1,0:T(8,128)S(1)}, f32[512,128]{1,0:T(8,128)S(1)}, u32[]{:S(2)}, u32[]{:S(2)}) collective-permute-start(f32[512,128]{1,0:T(8,128)S(1)} %get-tuple-element.25), channel_id=1, source_target_pairs={{0,8},{8,16},{16,24},{24,32},{32,40},{40,48},{48,56},{56,64},{64,7... | collective-permute-start | bytes 786440 | tf_op jit(solution)/shard_map/half_done/ppermute | solution.py:27
  50.4 10.4 %collective-permute-start.3 = (f32[512,128]{1,0:T(8,128)S(1)}, f32[512,128]{1,0:T(8,128)S(1)}, u32[]{:S(2)}, u32[]{:S(2)}) collective-permute-start(f32[512,128]{1,0:T(8,128)S(1)} %get-tuple-element.27), channel_id=1, source_target_pairs={{0,248},{8,0},{16,8},{24,16},{32,24},{40,32},{48,40},{56,48},{64,5... | collective-permute-start | bytes 786440 | tf_op jit(solution)/shard_map/half_done/ppermute | solution.py:27
  63.1 10.5 %collective-permute-start.4 = (f32[128,512]{1,0:T(8,128)S(1)}, f32[128,512]{1,0:T(8,128)S(1)}, u32[]{:S(2)}, u32[]{:S(2)}) collective-permute-start(f32[128,512]{1,0:T(8,128)S(1)} %get-tuple-element.29), channel_id=1, source_target_pairs={{0,8},{8,16},{16,24},{24,32},{32,40},{40,48},{48,56},{56,64},{64,7... | collective-permute-start | bytes 786440 | tf_op jit(solution)/shard_map/orthogonal/ppermute | solution.py:27
  63.2 11.3 %collective-permute-start.5 = (f32[128,512]{1,0:T(8,128)S(1)}, f32[128,512]{1,0:T(8,128)S(1)}, u32[]{:S(2)}, u32[]{:S(2)}) collective-permute-start(f32[128,512]{1,0:T(8,128)S(1)} %get-tuple-element.30), channel_id=1, source_target_pairs={{0,248},{8,0},{16,8},{24,16},{32,24},{40,32},{48,40},{56,48},{64,5... | collective-permute-start | bytes 786440 | tf_op jit(solution)/shard_map/orthogonal/ppermute | solution.py:27
  75.4 25.4 %collective-permute-start.6 = (f32[256,512]{1,0:T(8,128)}, f32[256,512]{1,0:T(8,128)}, u32[]{:S(2)}, u32[]{:S(2)}) collective-permute-start(f32[256,512]{1,0:T(8,128)} %get-tuple-element.41), channel_id=1, source_target_pairs={{0,2},{2,4},{4,6},{6,0},{1,3},{3,5},{5,7},{7,1},{8,10},{10,12},{12... | collective-permute-start | bytes 1572872 | tf_op jit(solution)/shard_map/orthogonal/ppermute | solution.py:27
  75.5 26.4 %collective-permute-start.7 = (f32[256,512]{1,0:T(8,128)}, f32[256,512]{1,0:T(8,128)S(1)}, u32[]{:S(2)}, u32[]{:S(2)}) collective-permute-start(f32[256,512]{1,0:T(8,128)} %get-tuple-element.41), channel_id=1, source_target_pairs={{0,6},{2,0},{4,2},{6,4},{1,7},{3,1},{5,3},{7,5},{8,14},{10,8},{12,... | collective-permute-start | bytes 1572872 | tf_op jit(solution)/shard_map/orthogonal/ppermute | solution.py:27
  78.1 39.1 %copy-start.10 = (s32[2]{0:T(128)S(1)}, s32[2]{0:T(128)}, u32[]{:S(2)}) copy-start(s32[2]{0:T(128)} %counts.1) | copy-start | bytes 28
  78.1 35.1 %collective-permute-start.10 = (f32[256,512]{1,0:T(8,128)}, f32[256,512]{1,0:T(8,128)S(1)}, u32[]{:S(2)}, u32[]{:S(2)}) collective-permute-start(f32[256,512]{1,0:T(8,128)} %get-tuple-element.41), channel_id=1, source_target_pairs={{0,1},{1,0},{2,3},{3,2},{4,5},{5,4},{6,7},{7,6},{8,9},{9,8},{10,11... | collective-permute-start | bytes 1572872 | tf_op jit(solution)/shard_map/orthogonal/ppermute | solution.py:27
  101.8 8.0 %collective-permute-start.8 = (f32[128,512]{1,0:T(8,128)S(1)}, f32[128,512]{1,0:T(8,128)S(1)}, u32[]{:S(2)}, u32[]{:S(2)}) collective-permute-start(f32[128,512]{1,0:T(8,128)S(1)} %slice.8), channel_id=1, source_target_pairs={{0,2},{2,4},{4,6},{6,0},{1,3},{3,5},{5,7},{7,1},{8,10},{10,12},{12... | collective-permute-start | bytes 786440 | tf_op jit(solution)/shard_map/orthogonal/ppermute | solution.py:27
  101.9 9.9 %collective-permute-start.9 = (f32[128,512]{1,0:T(8,128)S(1)}, f32[128,512]{1,0:T(8,128)S(1)}, u32[]{:S(2)}, u32[]{:S(2)}) collective-permute-start(f32[128,512]{1,0:T(8,128)S(1)} %slice.9), channel_id=1, source_target_pairs={{0,6},{2,0},{4,2},{6,4},{1,7},{3,1},{5,3},{7,5},{8,14},{10,8},{12,... | collective-permute-start | bytes 786440 | tf_op jit(solution)/shard_map/orthogonal/ppermute | solution.py:27
  104.7 9.3 %collective-permute-start.11 = (f32[256,512]{1,0:T(8,128)}, f32[256,512]{1,0:T(8,128)S(1)}, u32[]{:S(2)}, u32[]{:S(2)}) collective-permute-start(f32[256,512]{1,0:T(8,128)} %collective-permute-done.6), channel_id=1, source_target_pairs={{0,1},{1,0},{2,3},{3,2},{4,5},{5,4},{6,7},{7,6},{8,9},{9,8},{10,11... | collective-permute-start | bytes 1572872 | tf_op jit(solution)/shard_map/orthogonal/ppermute | solution.py:27
  106.4 8.5 %collective-permute-start.12 = (f32[256,512]{1,0:T(8,128)S(1)}, f32[256,512]{1,0:T(8,128)S(1)}, u32[]{:S(2)}, u32[]{:S(2)}) collective-permute-start(f32[256,512]{1,0:T(8,128)S(1)} %collective-permute-done.7), channel_id=1, source_target_pairs={{0,1},{1,0},{2,3},{3,2},{4,5},{5,4},{6,7},{7,6},{8,9},{9,8},{10,11... | collective-permute-start | bytes 1572872 | tf_op jit(solution)/shard_map/orthogonal/ppermute | solution.py:27
  109.7 6.0 %collective-permute-start.13 = (f32[128,512]{1,0:T(8,128)S(1)}, f32[128,512]{1,0:T(8,128)S(1)}, u32[]{:S(2)}, u32[]{:S(2)}) collective-permute-start(f32[128,512]{1,0:T(8,128)S(1)} %collective-permute-done.8), channel_id=1, source_target_pairs={{0,1},{1,0},{2,3},{3,2},{4,5},{5,4},{6,7},{7,6},{8,9},{9,8},{10,11... | collective-permute-start | bytes 786440 | tf_op jit(solution)/shard_map/orthogonal/ppermute | solution.py:27
  111.8 4.7 %collective-permute-start.14 = (f32[128,512]{1,0:T(8,128)S(1)}, f32[128,512]{1,0:T(8,128)S(1)}, u32[]{:S(2)}, u32[]{:S(2)}) collective-permute-start(f32[128,512]{1,0:T(8,128)S(1)} %collective-permute-done.9), channel_id=1, source_target_pairs={{0,1},{1,0},{2,3},{3,2},{4,5},{5,4},{6,7},{7,6},{8,9},{9,8},{10,11... | collective-permute-start | bytes 786440 | tf_op jit(solution)/shard_map/orthogonal/ppermute | solution.py:27
  117.2 1.9 %copy-start.4 = (f32[1536,512]{1,0:T(8,128)S(1)}, f32[1536,512]{1,0:T(8,128)}, u32[]{:S(2)}) copy-start(f32[1536,512]{1,0:T(8,128)} %all-gather.6.cloned.1.call-done.whole) | copy-start | bytes 9437188
  129.8 6.1 %collective-permute-start.15 = (f32[64,512]{1,0:T(8,128)S(1)}, f32[64,512]{1,0:T(8,128)S(1)}, u32[]{:S(2)}, u32[]{:S(2)}) collective-permute-start(f32[64,512]{1,0:T(8,128)S(1)} %solve.1), channel_id=1, source_target_pairs={{0,2},{2,4},{4,6},{6,0},{1,3},{3,5},{5,7},{7,1},{8,10},{10,12},{12... | collective-permute-start | bytes 393224 | tf_op jit(solution)/shard_map/share/ppermute | solution.py:27
  130.0 26.9 %copy-start.2 = (bf16[512,1536]{1,0:T(8,128)(2,1)S(1)}, bf16[512,1536]{1,0:T(8,128)(2,1)}, u32[]{:S(2)}) copy-start(bf16[512,1536]{1,0:T(8,128)(2,1)} %copy-done) | copy-start | bytes 4718596
  130.0 7.1 %collective-permute-start.16 = (f32[64,512]{1,0:T(8,128)S(1)}, f32[64,512]{1,0:T(8,128)S(1)}, u32[]{:S(2)}, u32[]{:S(2)}) collective-permute-start(f32[64,512]{1,0:T(8,128)S(1)} %solve.1), channel_id=1, source_target_pairs={{0,6},{2,0},{4,2},{6,4},{1,7},{3,1},{5,3},{7,5},{8,14},{10,8},{12,... | collective-permute-start | bytes 393224 | tf_op jit(solution)/shard_map/share/ppermute | solution.py:27
  132.9 7.0 %collective-permute-start.17 = (f32[64,512]{1,0:T(8,128)S(1)}, f32[64,512]{1,0:T(8,128)S(1)}, u32[]{:S(2)}, u32[]{:S(2)}) collective-permute-start(f32[64,512]{1,0:T(8,128)S(1)} %solve.1), channel_id=1, source_target_pairs={{0,4},{2,6},{4,0},{6,2},{1,5},{3,7},{5,1},{7,3},{8,12},{10,14},{12... | collective-permute-start | bytes 393224 | tf_op jit(solution)/shard_map/share/ppermute | solution.py:27
  134.1 6.9 %collective-permute-start.18 = (f32[64,512]{1,0:T(8,128)S(1)}, f32[64,512]{1,0:T(8,128)S(1)}, u32[]{:S(2)}, u32[]{:S(2)}) collective-permute-start(f32[64,512]{1,0:T(8,128)S(1)} %solve.1), channel_id=1, source_target_pairs={{0,1},{1,0},{2,3},{3,2},{4,5},{5,4},{6,7},{7,6},{8,9},{9,8},{10,11... | collective-permute-start | bytes 393224 | tf_op jit(solution)/shard_map/share/ppermute | solution.py:27
  135.8 5.3 %collective-permute-start.19 = (f32[64,512]{1,0:T(8,128)S(1)}, f32[64,512]{1,0:T(8,128)S(1)}, u32[]{:S(2)}, u32[]{:S(2)}) collective-permute-start(f32[64,512]{1,0:T(8,128)S(1)} %collective-permute-done.15), channel_id=1, source_target_pairs={{0,1},{1,0},{2,3},{3,2},{4,5},{5,4},{6,7},{7,6},{8,9},{9,8},{10,11... | collective-permute-start | bytes 393224 | tf_op jit(solution)/shard_map/share/ppermute | solution.py:27
  137.1 4.0 %collective-permute-start.20 = (f32[64,512]{1,0:T(8,128)S(1)}, f32[64,512]{1,0:T(8,128)S(1)}, u32[]{:S(2)}, u32[]{:S(2)}) collective-permute-start(f32[64,512]{1,0:T(8,128)S(1)} %collective-permute-done.16), channel_id=1, source_target_pairs={{0,1},{1,0},{2,3},{3,2},{4,5},{5,4},{6,7},{7,6},{8,9},{9,8},{10,11... | collective-permute-start | bytes 393224 | tf_op jit(solution)/shard_map/share/ppermute | solution.py:27
  139.9 2.2 %collective-permute-start.21 = (f32[64,512]{1,0:T(8,128)S(1)}, f32[64,512]{1,0:T(8,128)S(1)}, u32[]{:S(2)}, u32[]{:S(2)}) collective-permute-start(f32[64,512]{1,0:T(8,128)S(1)} %collective-permute-done.17), channel_id=1, source_target_pairs={{0,1},{1,0},{2,3},{3,2},{4,5},{5,4},{6,7},{7,6},{8,9},{9,8},{10,11... | collective-permute-start | bytes 393224 | tf_op jit(solution)/shard_map/share/ppermute | solution.py:27
  142.1 1.1 copy-start.8
  146.0 10.9 %collective-permute-start.22 = (f32[512,128]{1,0:T(8,128)S(1)}, f32[512,128]{1,0:T(8,128)S(1)}, u32[]{:S(2)}, u32[]{:S(2)}) collective-permute-start(f32[512,128]{1,0:T(8,128)S(1)} %get-tuple-element.31), channel_id=1, source_target_pairs={{0,8},{8,16},{16,24},{24,32},{32,40},{40,48},{48,56},{56,64},{64,7... | collective-permute-start | bytes 786440 | tf_op jit(solution)/shard_map/half_back/ppermute | solution.py:27
  146.1 10.8 %collective-permute-start.23 = (f32[512,128]{1,0:T(8,128)S(1)}, f32[512,128]{1,0:T(8,128)S(1)}, u32[]{:S(2)}, u32[]{:S(2)}) collective-permute-start(f32[512,128]{1,0:T(8,128)S(1)} %get-tuple-element.33), channel_id=1, source_target_pairs={{0,248},{8,0},{16,8},{24,16},{32,24},{40,32},{48,40},{56,48},{64,5... | collective-permute-start | bytes 786440 | tf_op jit(solution)/shard_map/half_back/ppermute | solution.py:27
Sparse Core Ops, SparseCore 0:
  9.8 34.5 all-gather.3
  63.3 38.8 all-gather.5
